TPU v7x, 128 devices: a whole 4x4x4 slice. The times are simulated.
128 devices in a mesh: sx: 8 (over y, z_lo), sz: 16 (over x, z_hi, core).
Axes of the slice: x: 4, y: 4, z: 4 (z_hi: 2, z_lo: 2; z = z_hi * 2 + z_lo), core: 2. Of those that a mesh axis runs over, the one named last changes fastest.
Arguments:
- right_side: float32 [72, 256, 4096], P('sx', 'sz'), may hold values from -6 to 6
- coupling: bfloat16 [72, 5, 256, 256], P('sx'), may hold values from -0.15625 to 0.15625
- harmonic_offsets: int32 [5], replicated, may hold values from -6 to 6, as said below
- eigen_basis: bfloat16 [256, 256], replicated, may hold values from -0.375 to 0.375
- eigen_inverse: bfloat16 [256, 256], replicated, may hold values from -0.375 to 0.375
- eigen_size: float32 [256], replicated, may hold values from 0.5 to 50
Outputs:
- solution: float32 [72, 256, 4096], P('sx', 'sz')
Inputs may be any that keep to these rules, and one draw needn't show every extreme that they name: `harmonic_offsets`: the offsets are distinct; some offset equals 6 and some equals -6.
All inputs are finite; a program needn't handle non-finite values.
Results may differ from a plain program's by a relative error of at most 0.00065.
The roundings to bfloat16 on the way count: a program that leaves them out, or rounds other values in their place, can miss the bound.
Values may be sent and summed in bfloat16 or wider, within the bound.
A program may use at most 128 MiB of HBM per device.

v0:
```python
import jax
import jax.numpy as jnp
from jax import lax
from jax.sharding import PartitionSpec as P

KX = 72
KZ = 128
H = 5
OFF = 6
STEPS = 2
R = 32


def extended(value, sides, width):
    for axis, dim in sides:
        peers, length = (lax.axis_size(axis), value.shape[dim])
        up = [(i, (i + 1) % peers) for i in range(peers)]
        down = [(j, i) for i, j in up]
        last = lax.slice_in_dim(value, length - width, length, axis=dim)
        first = lax.slice_in_dim(value, 0, width, axis=dim)
        before = lax.ppermute(last, axis, up)
        after = lax.ppermute(first, axis, down)
        value = jnp.concatenate([before, value, after], axis=dim)
    return value


def wave_table(mode_count, span_count):
    first_mode = lax.axis_index("sx") * mode_count
    first_span = lax.axis_index("sz") * span_count
    modes = first_mode + jnp.arange(mode_count, dtype=jnp.int32)
    spans = first_span + jnp.arange(span_count, dtype=jnp.int32)
    signed_x = jnp.where(modes < KX // 2, modes, modes - KX).astype(jnp.float32) * (4.0 / KX)
    signed_z = jnp.where(spans < KZ // 2, spans, spans - KZ).astype(jnp.float32) * (4.0 / KZ)
    table = 1.0 + signed_x[:, None] ** 2 + signed_z[None, :] ** 2
    return jnp.repeat(table, R, axis=1)


def precondition(residual, eigen_basis, eigen_inverse, eigen_size, wave_square):
    rounded = residual.astype(jnp.bfloat16)
    spectral = jnp.einsum("ij,kjc->kic", eigen_inverse, rounded, preferred_element_type=jnp.float32)
    factor = -1.0 / (eigen_size[None, :, None] + wave_square[:, None, :])
    scaled = (spectral * factor).astype(jnp.bfloat16)
    result = jnp.einsum("ij,kjc->kic", eigen_basis, scaled, preferred_element_type=jnp.float32)
    return result.astype(jnp.bfloat16)


def apply_operator(search, coupling, harmonic_offsets, wave_square):
    mode_count = search.shape[0]
    padded = extended(search, (("sx", 0),), OFF)
    accum = -wave_square[:, None, :] * search.astype(jnp.float32)
    for harmonic in range(H):
        source = lax.dynamic_slice_in_dim(padded, OFF + harmonic_offsets[harmonic], mode_count, 0)
        accum = accum + jnp.einsum(
            "kij,kjc->kic", coupling[:, harmonic], source, preferred_element_type=jnp.float32
        )
    return accum


def relax(solution, residual, search_full, image):
    inner = jnp.sum(jnp.sum(image * residual, axis=(0, 1)).reshape(-1, R), axis=0)
    energy = jnp.sum(jnp.sum(image * image, axis=(0, 1)).reshape(-1, R), axis=0)
    aligned, total_energy = lax.psum((inner, energy), ("sx", "sz"))
    step_size = jnp.tile(aligned / (total_energy + 1e-06), image.shape[2] // R)
    return (solution + step_size * search_full, residual - step_size * image)


def shards(right_side, coupling, harmonic_offsets, eigen_basis, eigen_inverse, eigen_size):
    residual = lax.all_to_all(right_side, "sz", split_axis=2, concat_axis=1, tiled=True)
    wave_square = wave_table(residual.shape[0], residual.shape[2] // R)
    solution = jnp.zeros_like(residual)
    for sweep in range(STEPS):
        search = precondition(residual, eigen_basis, eigen_inverse, eigen_size, wave_square)
        image = apply_operator(search, coupling, harmonic_offsets, wave_square)
        solution, residual = relax(solution, residual, search.astype(jnp.float32), image)
    return lax.all_to_all(solution, "sz", split_axis=1, concat_axis=2, tiled=True)


def solution(mesh):
    in_specs = (P("sx", "sz", None), P("sx", None, None, None), P(), P(), P(), P())
    out_specs = P("sx", "sz", None)
    return jax.shard_map(shards, mesh=mesh, in_specs=in_specs, out_specs=out_specs, check_vma=False)
```

profile of v0, /device:TPU:1, one launch (start us, length us, event | category | flops | bytes accessed | tf_op | source)
XLA Modules:
  0.0 424.5 jit_solution(962264210277215487)
XLA Ops:
  0.0 17.6 %copy.68 = f32[9,16,4096]{1,0,2:T(8,128)} copy(f32[9,16,4096]{2,1,0:T(8,128)} %param.6) | data formatting | bytes 4718592 | tf_op args[0]
  17.6 19.3 %reshape.75 = f32[16,1,36864]{2,1,0:T(1,128)} reshape(f32[4096,9,16]{2,1,0:T(8,128)} %bitcast.113) | data formatting | bytes 4718592
  36.9 9.1 %all-to-all-start = ((f32[16,1,36864]{2,1,0:T(1,128)}), f32[16,1,36864]{2,1,0:T(1,128)S(1)}, u32[]{:S(2)}, u32[]{:S(2)}) async-start(f32[16,1,36864]{2,1,0:T(1,128)} %reshape.75), calls=%async_computation | async-start | bytes 4718592 | tf_op jit(solution)/shard_map/all_to_all | solution.py:68
  46.2 0.1 broadcast_in_dim_reshape.2
  46.3 31.0 %all-to-all-done = f32[16,1,36864]{2,1,0:T(1,128)S(1)} async-done(((f32[16,1,36864]{2,1,0:T(1,128)}), f32[16,1,36864]{2,1,0:T(1,128)S(1)}, u32[]{:S(2)}, u32[]{:S(2)}) %all-to-all-start) | async-done | bytes 2359328 | tf_op jit(solution)/shard_map/all_to_all | solution.py:68
  77.3 1.4 copy-done.4
  78.7 0.6 broadcast.95
  79.3 8.0 %reduce = f32[16,36864]{1,0:T(8,128)S(1)} reduce(f32[16,1,36864]{2,1,0:T(1,128)} %copy-done.4, f32[]{:T(128)} %broadcast.95), dimensions={1}, to_apply=%all_to_all.26.reduce_sub_computation | reduce | bytes 4718596 | tf_op jit(solution)/shard_map/all_to_all | solution.py:68
  87.3 21.2 %reshape.76 = f32[4096,9,16]{2,1,0:T(8,128)} reshape(f32[16,36864]{1,0:T(8,128)S(1)} %reduce) | data formatting | bytes 4718592
  108.5 18.9 %copy.70 = f32[9,16,16,256]{3,2,1,0:T(8,128)S(1)} copy(f32[9,16,16,256]{2,0,3,1:T(8,128)} %bitcast.112) | data formatting | bytes 4718592 | tf_op jit(solution)/shard_map/all_to_all | solution.py:68
  127.4 1.5 copy.71
  128.9 3.3 fusion.13
  132.2 2.4 fusion.89
  134.6 0.7 collective-permute-start
  135.3 2.8 collective-permute-start.1
  138.1 0.7 fusion.90
  145.0 23.4 %collective-permute-done = bf16[6,256,256]{2,1,0:T(8,128)(2,1)} collective-permute-done((bf16[6,256,256]{2,1,0:T(8,128)(2,1)}, bf16[6,256,256]{2,1,0:T(8,128)(2,1)}, u32[]{:S(2)}, u32[]{:S(2)}) %collective-permute-start) | collective-permute-done | bytes 786464 | tf_op jit(solution)/shard_map/ppermute | solution.py:21
  168.4 2.3 collective-permute-done.1
  170.7 2.2 pad_maximum_fusion
  172.9 1.9 fusion.21
  174.8 1.8 fusion.25
  176.6 0.5 fusion.29
  177.0 0.5 fusion.17
  177.5 0.8 copy-done.1
  178.3 2.7 multiply_reduce_fusion.2
  181.2 67.8 %all-reduce.1 = (f32[32]{0:T(128)S(1)}, f32[32]{0:T(128)S(1)}) all-reduce(f32[32]{0:T(128)S(1)} %reduce_sum.73, f32[32]{0:T(128)S(1)} %reduce_sum.75), channel_id=1, replica_groups=mesh['sx'=8,'sz'=16] {'sx','sz'}, use_global_device_ids=true, to_apply=%region_2.3 | all-reduce | flops 64 | bytes 512 | tf_op jit(solution)/shard_map/psum | solution.py:62
  249.0 0.1 mul.87
  249.1 3.8 fusion.14
  252.9 1.6 fusion.88
  254.5 0.3 collective-permute-start.2
  254.8 3.3 collective-permute-start.3
  258.2 29.7 %collective-permute-done.2 = bf16[6,256,256]{2,1,0:T(8,128)(2,1)S(1)} collective-permute-done((bf16[6,256,256]{2,1,0:T(8,128)(2,1)S(1)}, bf16[6,256,256]{2,1,0:T(8,128)(2,1)S(1)}, u32[]{:S(2)}, u32[]{:S(2)}) %collective-permute-start.2) | collective-permute-done | bytes 786464 | tf_op jit(solution)/shard_map/ppermute | solution.py:21
  287.9 1.9 collective-permute-done.3
  289.8 1.6 pad_maximum_fusion.1
  291.4 1.8 fusion.23
  293.2 0.5 fusion.27
  293.7 0.5 fusion.31
  294.2 0.5 fusion.19
  294.6 0.8 copy-done.2
  295.4 0.8 copy-done.3
  296.2 1.5 multiply_reduce_fusion
  297.9 65.3 %all-reduce = (f32[32]{0:T(128)S(1)}, f32[32]{0:T(128)S(1)}) all-reduce(f32[32]{0:T(128)S(1)} %reduce_sum.77, f32[32]{0:T(128)S(1)} %reduce_sum.79), channel_id=1, replica_groups=mesh['sx'=8,'sz'=16] {'sx','sz'}, use_global_device_ids=true, to_apply=%region_8.9 | all-reduce | flops 64 | bytes 512 | tf_op jit(solution)/shard_map/psum | solution.py:62
  363.2 0.1 mul.95
  363.3 2.0 fusion.5
  365.3 1.5 copy.80
  366.8 54.6 %all_to_all.36 = f32[9,256,256]{2,0,1:T(8,128)S(1)} all-to-all(f32[9,256,256]{2,0,1:T(8,128)S(1)} %copy.80), channel_id=1, replica_groups=mesh['sx'=8,'sz'=16] {'sz'}, dimensions={1} | all-to-all | bytes 4718592 | tf_op jit(solution)/shard_map/all_to_all | solution.py:75
  421.5 1.4 copy.81
  422.8 1.6 all_to_all.33
  (39 shorter events, 0.6 us)
Async XLA Ops:
  0.0 128.9 %copy-start = (bf16[256,256]{1,0:T(8,128)(2,1)S(1)}, bf16[256,256]{1,0:T(8,128)(2,1)}, u32[]{:S(2)}) copy-start(bf16[256,256]{1,0:T(8,128)(2,1)} %param.9) | copy-start | bytes 393220
  36.9 40.4 %all-to-all-start = ((f32[16,1,36864]{2,1,0:T(1,128)}), f32[16,1,36864]{2,1,0:T(1,128)S(1)}, u32[]{:S(2)}, u32[]{:S(2)}) async-start(f32[16,1,36864]{2,1,0:T(1,128)} %reshape.75), calls=%async_computation | async-start | bytes 4718592 | tf_op jit(solution)/shard_map/all_to_all | solution.py:68
  77.3 1.4 copy-start.4
  127.4 1.5 copy-start.6
  127.4 1.5 copy-start.7
  132.2 5.9 %copy-start.5 = (s32[5]{0:T(128)S(1)}, s32[5]{0:T(128)}, u32[]{:S(2)}) copy-start(s32[5]{0:T(128)} %param.8) | copy-start | bytes 64
  134.6 33.8 %collective-permute-start = (bf16[6,256,256]{2,1,0:T(8,128)(2,1)}, bf16[6,256,256]{2,1,0:T(8,128)(2,1)}, u32[]{:S(2)}, u32[]{:S(2)}) collective-permute-start(bf16[6,256,256]{2,1,0:T(8,128)(2,1)} %get-tuple-element.15), channel_id=1, source_target_pairs={{0,16},{16,32},{32,48},{48,64},{64,80},{80,96},{96,112},{112,0},{1... | collective-permute-start | bytes 2359304 | tf_op jit(solution)/shard_map/ppermute | solution.py:21
  135.3 35.4 %collective-permute-start.1 = (bf16[6,256,256]{2,1,0:T(8,128)(2,1)S(1)}, bf16[6,256,256]{2,1,0:T(8,128)(2,1)}, u32[]{:S(2)}, u32[]{:S(2)}) collective-permute-start(bf16[6,256,256]{2,1,0:T(8,128)(2,1)S(1)} %get-tuple-element.16), channel_id=1, source_target_pairs={{16,0},{32,16},{48,32},{64,48},{80,64},{96,80},{112,96},{0,112},{1... | collective-permute-start | bytes 2359304 | tf_op jit(solution)/shard_map/ppermute | solution.py:22
  170.7 5.9 %slice-start = ((s8[5898240]{0:T(1024)(128)(4,1)}), s8[4194304]{0:T(1024)(128)(4,1)S(1)}, s32[]{:S(2)}) async-start(s8[5898240]{0:T(1024)(128)(4,1)} %bitcast.116), calls=%async_computation.2 | async-start | bytes 8388608
  172.9 3.7 slice-start.1
  177.0 1.3 copy-start.1
  252.9 40.3 %slice-start.2 = ((s8[5898240]{0:T(1024)(128)(4,1)}), s8[4194304]{0:T(1024)(128)(4,1)S(1)}, s32[]{:S(2)}) async-start(s8[5898240]{0:T(1024)(128)(4,1)} %bitcast.118), calls=%async_computation.4 | async-start | bytes 8388608
  254.5 33.4 %collective-permute-start.2 = (bf16[6,256,256]{2,1,0:T(8,128)(2,1)S(1)}, bf16[6,256,256]{2,1,0:T(8,128)(2,1)S(1)}, u32[]{:S(2)}, u32[]{:S(2)}) collective-permute-start(bf16[6,256,256]{2,1,0:T(8,128)(2,1)S(1)} %get-tuple-element.13), channel_id=1, source_target_pairs={{0,16},{16,32},{32,48},{48,64},{64,80},{80,96},{96,112},{112,0},{1... | collective-permute-start | bytes 2359304 | tf_op jit(solution)/shard_map/ppermute | solution.py:21
  254.8 38.3 %slice-start.3 = ((s8[5898240]{0:T(1024)(128)(4,1)}), s8[1703936]{0:T(1024)(128)(4,1)S(1)}, s32[]{:S(2)}) async-start(s8[5898240]{0:T(1024)(128)(4,1)} %bitcast.118), calls=%async_computation.5 | async-start | bytes 3407872
  254.8 35.0 %collective-permute-start.3 = (bf16[6,256,256]{2,1,0:T(8,128)(2,1)S(1)}, bf16[6,256,256]{2,1,0:T(8,128)(2,1)S(1)}, u32[]{:S(2)}, u32[]{:S(2)}) collective-permute-start(bf16[6,256,256]{2,1,0:T(8,128)(2,1)S(1)} %get-tuple-element.14), channel_id=1, source_target_pairs={{16,0},{32,16},{48,32},{64,48},{80,64},{96,80},{112,96},{0,112},{1... | collective-permute-start | bytes 2359304 | tf_op jit(solution)/shard_map/ppermute | solution.py:22
  294.1 1.3 copy-start.2
  294.1 2.0 copy-start.3
where the time goes:
time: 426 us; the launch traced here: 424 us
  blocking collectives  188 us (44%)
  local copies, waits for them, and re-layouts  92.6 us (22%)
  waiting for transfers between devices  88.3 us (21%)
  matrix products  19.1 us (4%)
  starting transfers between devices  16.3 us (4%)
  other arithmetic  13.9 us (3%)
  between operations  6.39 us (2%)
    psum x2, blocking collectives, relax(): aligned, total_energy = lax.psum((inner, energy), ('sx', 'sz'))  133 us
    unnamed x27, local copies, waits for them, and re-layouts  61.9 us
    all_to_all x1, blocking collectives, shards(): lax.all_to_all(solution, 'sz', split_axis=1, concat_axis=2, tiled=True)  54.6 us
    ppermute x2, waiting for transfers between devices, extended(): before = lax.ppermute(last, axis, up)  53.1 us
    all_to_all x1, waiting for transfers between devices, shards(): lax.all_to_all(right_side, 'sz', split_axis=2, concat_axis=1, tiled=True)  31 us
    all_to_all x3, local copies, waits for them, and re-layouts, shards(): lax.all_to_all(right_side, 'sz', split_axis=2, concat_axis=1, tiled=True)  21 us
    dot_general x10, matrix products, apply_operator(): jnp.einsum('kij,kjc->kic', coupling[:, harmonic], source, preferred_eleme...  12 us
    all_to_all x1, starting transfers between devices, shards(): lax.all_to_all(right_side, 'sz', split_axis=2, concat_axis=1, tiled=True)  9.13 us
  transfers between devices with their start and end apart: 5, of which 5 were waited for; matrix products, arithmetic and copies ran while one was open for 0% of the time, Pallas kernels for 0%

commit v1 on v0

v1 whole, which is shorter than its diff:
```python
import jax
import jax.numpy as jnp
from jax import lax
from jax.experimental import pallas as pl
from jax.experimental.pallas import tpu as pltpu
from jax.sharding import PartitionSpec as P

KX = 72
KZ = 128
NC = 256
H = 5
OFF = 6
R = 32
NX = 8
NZ = 16
M = KX // NX
ROWS = NC // NZ
COLS = KZ * R // NZ
SPANS = KZ // NZ
MESH = pl.DeviceIdType.MESH
PARTS_OF = ((0,), (1, 2), (3,))

CHUNK = 3
CHUNKS = M // CHUNK


def flip(place):
    return 2 - 4 * ((place // 2) % 2)


def group_of(sx, sz):
    return sz + ((sx // 2) % 2) * flip(sz)


def wave_row(sx, mode, group):
    index = sx * M + mode
    signed_x = jnp.where(index < KX // 2, index, index - KX).astype(jnp.float32) * (4.0 / KX)
    column = lax.broadcasted_iota(jnp.int32, (1, COLS), 1)
    span = group * SPANS + column // R
    signed_z = jnp.where(span < KZ // 2, span, span - KZ).astype(jnp.float32) * (4.0 / KZ)
    return 1.0 + signed_x * signed_x + signed_z * signed_z


def kernel(
    offsets, right, coupling, basis, inverse, sizes, out,
    start, factor, image, residual, blocks,
    search, back, final, sums, parts, row_sums, row_total, all_sums,
    load_sem, in_send, in_recv, move_send, move_recv, halo_send, halo_recv, row_send, row_recv, all_send, all_recv, local_sem, out_sem,
):
    sx, sz = lax.axis_index("sx"), lax.axis_index("sz")
    low_z = sx % 2
    group = group_of(sx, sz)
    up = ((sx + 1) % NX, sz + low_z * flip(sz))
    down = ((sx + NX - 1) % NX, sz + (1 - low_z) * flip(sz))
    twisted = (low_z * up[0] + (1 - low_z) * down[0], sz + flip(sz))

    load_blocks = pltpu.make_async_copy(coupling, blocks, load_sem.at[0])
    load_blocks.start()

    barrier = pltpu.get_barrier_semaphore()

    @pl.loop(1, NZ)
    def _(k):
        pl.semaphore_signal(barrier, inc=1, device_id=(sx, (sz + k) % NZ), device_id_type=MESH)

    @pl.loop(1, NX)
    def _(k):
        pl.semaphore_signal(barrier, inc=1, device_id=((sx + k) % NX, sz), device_id_type=MESH)

    pl.semaphore_signal(barrier, inc=1, device_id=twisted, device_id_type=MESH)

    pl.semaphore_wait(barrier, NZ - 1 + NX - 1 + 1)

    def columns(place):
        return pl.ds(pl.multiple_of(place * COLS, COLS), COLS)

    def rows(place):
        return pl.ds(pl.multiple_of(place * ROWS, ROWS), ROWS)

    def modes(chunk):
        return pl.ds(chunk * CHUNK, CHUNK)

    def inward(chunk, k):
        to = (sz + k) % NZ
        return pltpu.make_async_remote_copy(
            src_ref=right.at[modes(chunk), :, columns(group_of(sx, to))],
            dst_ref=start.at[modes(chunk), rows(sz), :],
            send_sem=in_send.at[chunk, k],
            recv_sem=in_recv.at[chunk, k],
            device_id=(sx, to),
            device_id_type=MESH,
        )

    def outward(step, k):
        to = (sz + k) % NZ
        return pltpu.make_async_remote_copy(
            src_ref=search.at[step, pl.ds(OFF, M), rows(to), :],
            dst_ref=back.at[step, :, :, columns(group)],
            send_sem=move_send.at[step, k],
            recv_sem=move_recv.at[step, k],
            device_id=(sx, to),
            device_id_type=MESH,
        )

    def halo(step, part):
        to, begin, end = (
            (down, 0, M), (down, 3, M + 3), (up, 3, -OFF + 0), (up, 6, -OFF + 3),
        )[part]
        return pltpu.make_async_remote_copy(
            src_ref=search.at[step, pl.ds(OFF + begin, 3)],
            dst_ref=search.at[step, pl.ds(OFF + end, 3)],
            send_sem=halo_send.at[step, part],
            recv_sem=halo_recv.at[step, part],
            device_id=to,
            device_id_type=MESH,
        )

    for chunk in range(CHUNKS):

        @pl.loop(1, NZ)
        def _(k):
            inward(chunk, k).start()

    own = pltpu.make_async_copy(right.at[:, :, columns(group)], start.at[:, rows(sz), :], local_sem.at[0])
    own.start()

    @pl.loop(0, M)
    def _(m):
        factor[m] = -1.0 / (sizes[...] + wave_row(sx, m, group))

    own.wait()

    def precondition(step, m, rounded):
        spectral = jnp.dot(inverse[...], rounded, preferred_element_type=jnp.float32)
        scaled = (spectral * factor[m]).astype(jnp.bfloat16)
        result = jnp.dot(basis[...], scaled, preferred_element_type=jnp.float32)
        search[step, OFF + m] = result.astype(jnp.bfloat16)

    def apply(step):
        for part in range(4):
            halo(step, part).wait_recv()
        sums[...] = jnp.zeros_like(sums)

        @pl.loop(0, M)
        def _(m):
            total = -wave_row(sx, m, group) * search[step, OFF + m].astype(jnp.float32)
            for h in range(H):
                total = total + jnp.dot(
                    blocks[m, h], search[step, OFF + m + offsets[h]], preferred_element_type=jnp.float32
                )
            if step == 0:
                image[m] = total
                before = start[m]
            else:
                before = residual[m]
            sums[0] += jnp.sum((total * before).reshape(NC // 8, 8, COLS), axis=0)
            sums[1] += jnp.sum((total * total).reshape(NC // 8, 8, COLS), axis=0)

    def row_copy(step, k):
        to = (sz + k) % NZ
        return pltpu.make_async_remote_copy(
            src_ref=parts.at[step],
            dst_ref=row_sums.at[step, sz],
            send_sem=row_send.at[step, k],
            recv_sem=row_recv.at[step, k],
            device_id=(sx, to),
            device_id_type=MESH,
        )

    def all_copy(step, k):
        to = (sx + k) % NX
        return pltpu.make_async_remote_copy(
            src_ref=row_total.at[step],
            dst_ref=all_sums.at[step, sx],
            send_sem=all_send.at[step, k],
            recv_sem=all_recv.at[step, k],
            device_id=(to, sz),
            device_id_type=MESH,
        )

    first_half = lax.broadcasted_iota(jnp.int32, (8, 128), 1) < 64

    def step_size(step):
        def fold(value):
            value = value[:, :128] + value[:, 128:]
            value = value + pltpu.roll(value, 64, 1)
            return value + pltpu.roll(value, 32, 1)

        both = jnp.where(first_half, fold(sums[0]), fold(sums[1]))
        mine = jnp.sum(both, axis=0, keepdims=True)
        parts[step] = mine
        row_sums[step, sz] = mine

        @pl.loop(1, NZ)
        def _(k):
            row_copy(step, k).start()

        @pl.loop(1, NZ)
        def _(k):
            row_copy(step, k).wait_recv()

        of_row = row_sums[step, 0]
        for place in range(1, NZ):
            of_row = of_row + row_sums[step, place]
        row_total[step] = of_row
        all_sums[step, sx] = of_row

        @pl.loop(1, NX)
        def _(k):
            all_copy(step, k).start()

        @pl.loop(1, NX)
        def _(k):
            all_copy(step, k).wait_recv()

        of_all = all_sums[step, 0]
        for place in range(1, NX):
            of_all = of_all + all_sums[step, place]
        of_all = jnp.broadcast_to(of_all, (8, 128))
        other = pltpu.roll(of_all, 64, 1)
        aligned = jnp.where(first_half, of_all, other)
        energy = jnp.where(first_half, other, of_all)
        return (aligned / (energy + 1e-6))[0:1]

    for chunk in range(CHUNKS):

        @pl.loop(1, NZ)
        def _(k):
            inward(chunk, k).wait_recv()

        @pl.loop(chunk * CHUNK, chunk * CHUNK + CHUNK)
        def _(m):
            precondition(0, m, start[m].astype(jnp.bfloat16))

        for part in PARTS_OF[chunk]:
            halo(0, part).start()

    @pl.loop(1, NZ)
    def _(k):
        outward(0, k).start()

    own_first = pltpu.make_async_copy(
        search.at[0, pl.ds(OFF, M), rows(sz), :], back.at[0, :, :, columns(group)], local_sem.at[1]
    )
    own_first.start()

    load_blocks.wait()

    apply(0)
    first = step_size(0)
    first_wide = jnp.concatenate([first, first], axis=1)

    for chunk in range(CHUNKS):

        @pl.loop(chunk * CHUNK, chunk * CHUNK + CHUNK)
        def _(m):
            left = start[m] - first_wide * image[m]
            residual[m] = left
            precondition(1, m, left.astype(jnp.bfloat16))

        for part in PARTS_OF[chunk]:
            halo(1, part).start()

    @pl.loop(1, NZ)
    def _(k):
        outward(1, k).start()

    own_second = pltpu.make_async_copy(
        search.at[1, pl.ds(OFF, M), rows(sz), :], back.at[1, :, :, columns(group)], local_sem.at[2]
    )
    own_second.start()
    apply(1)
    second = step_size(1)

    own_first.wait()
    own_second.wait()

    @pl.loop(1, NZ)
    def _(k):
        outward(0, k).wait_recv()
        outward(1, k).wait_recv()

    reach = KZ * R // 128
    first_all = jnp.tile(first, (1, reach))
    second_all = jnp.tile(second, (1, reach))

    @pl.loop(0, M)
    def _(m):
        final[m] = first_all * back[0, m].astype(jnp.float32) + second_all * back[1, m].astype(jnp.float32)
        pltpu.make_async_copy(final.at[m], out.at[m], out_sem.at[m]).start()

    @pl.loop(1, NZ)
    def _(k):
        for chunk in range(CHUNKS):
            inward(chunk, k).wait_send()
        outward(0, k).wait_send()
        outward(1, k).wait_send()
        row_copy(0, k).wait_send()
        row_copy(1, k).wait_send()

    @pl.loop(1, NX)
    def _(k):
        all_copy(0, k).wait_send()
        all_copy(1, k).wait_send()

    for step in range(2):
        for part in range(4):
            halo(step, part).wait_send()

    @pl.loop(0, M)
    def _(m):
        pltpu.make_async_copy(final.at[m], out.at[m], out_sem.at[m]).wait()


def shards(right_side, coupling, harmonic_offsets, eigen_basis, eigen_inverse, eigen_size):
    vmem = pl.BlockSpec(memory_space=pltpu.VMEM)
    anywhere = pl.BlockSpec(memory_space=pl.ANY)
    low, full = jnp.bfloat16, jnp.float32
    dma = pltpu.SemaphoreType.DMA
    return pl.pallas_call(
        kernel,
        out_shape=jax.ShapeDtypeStruct((M, ROWS, KZ * R), full),
        in_specs=[pl.BlockSpec(memory_space=pltpu.SMEM), anywhere, anywhere, vmem, vmem, vmem],
        out_specs=anywhere,
        scratch_shapes=[
            pltpu.VMEM((M, NC, COLS), full),
            pltpu.VMEM((M, NC, COLS), full),
            pltpu.VMEM((M, NC, COLS), full),
            pltpu.VMEM((M, NC, COLS), full),
            pltpu.VMEM((M, H, NC, NC), low),
            pltpu.VMEM((2, M + 2 * OFF, NC, COLS), low),
            pltpu.VMEM((2, M, ROWS, KZ * R), low),
            pltpu.VMEM((M, ROWS, KZ * R), full),
            pltpu.VMEM((2, 8, COLS), full),
            pltpu.VMEM((2, 1, 128), full),
            pltpu.VMEM((2, NZ, 1, 128), full),
            pltpu.VMEM((2, 1, 128), full),
            pltpu.VMEM((2, NX, 1, 128), full),
            dma((1,)),
            dma((CHUNKS, NZ)),
            dma((CHUNKS, NZ)),
            dma((2, NZ)),
            dma((2, NZ)),
            dma((2, 4)),
            dma((2, 4)),
            dma((2, NZ)),
            dma((2, NZ)),
            dma((2, NX)),
            dma((2, NX)),
            dma((3,)),
            dma((M,)),
        ],
        compiler_params=pltpu.CompilerParams(
            collective_id=0, has_side_effects=True, vmem_limit_bytes=56 * 2**20
        ),
    )(harmonic_offsets, right_side, coupling, eigen_basis, eigen_inverse, eigen_size.reshape(NC, 1))


def solution(mesh):
    in_specs = (P("sx", "sz", None), P("sx", None, None, None), P(), P(), P(), P())
    out_specs = P("sx", "sz", None)
    return jax.shard_map(shards, mesh=mesh, in_specs=in_specs, out_specs=out_specs, check_vma=False)
```

time: 426 us -> 139 us (0.33)
  blocking collectives: 188 us -> 0 us
  Pallas kernels: 0 us -> 134 us
  waiting for transfers between devices: 88.3 us -> 0 us
  local copies, waits for them, and re-layouts: 92.6 us -> 4.75 us
  matrix products: 19.1 us -> 0 us
  starting transfers between devices: 16.3 us -> 0 us
  other arithmetic: 13.9 us -> 0 us
  between operations: 6.39 us -> 0.01 us
    pallas_call x0 -> x1, Pallas kernels: none -> 134 us  [shards(): pl.pallas_call(kernel, out_shape=jax.ShapeDtypeStruct((M, ROWS, KZ * R),...]
    psum x2 -> x0, blocking collectives: 133 us -> none  [relax(): aligned, total_energy = lax.psum((inner, energy), ('sx', 'sz'))]
    unnamed x27 -> x1, local copies, waits for them, and re-layouts: 61.9 us -> 3.27 us
    ppermute x4 -> x0, waiting for transfers between devices: 57.3 us -> none  [the longest x2 53.1 us: extended(): before = lax.ppermute(last, axis, up)]
    all_to_all x1 -> x0, blocking collectives: 54.6 us -> none  [shards(): lax.all_to_all(solution, 'sz', split_axis=1, concat_axis=2, tiled=True)]
    all_to_all x1 -> x0, waiting for transfers between devices: 31 us -> none  [shards(): lax.all_to_all(right_side, 'sz', split_axis=2, concat_axis=1, tiled=True)]
    all_to_all x5 -> x0, local copies, waits for them, and re-layouts: 24 us -> none  [the longest x3 21 us: shards(): lax.all_to_all(right_side, 'sz', split_axis=2, concat_axis=1, tiled=True)]
    dot_general x12 -> x0, matrix products: 19.1 us -> none  [the longest x10 12 us: apply_operator(): jnp.einsum('kij,kjc->kic', coupling[:, harmonic], source, preferred_eleme...]
  transfers between devices with their start and end apart: 5 -> 0, of which waited for: 5 -> 0; matrix products, arithmetic and copies ran while one was open for 0% -> 0% of each run, Pallas kernels for 0% -> 0%
where the time goes in v1:
time: 139 us; the launch traced here: 138 us
  Pallas kernels  134 us (96%)
  local copies, waits for them, and re-layouts  4.75 us (3%)
    pallas_call x1, Pallas kernels, shards(): pl.pallas_call(kernel, out_shape=jax.ShapeDtypeStruct((M, ROWS, KZ * R),...  134 us
    unnamed x1, local copies, waits for them, and re-layouts  3.27 us

profile of v1, /device:TPU:1, one launch (start us, length us, event | category | flops | bytes accessed | tf_op | source)
XLA Modules:
  0.0 138.5 jit_solution(12136958160361558223)
XLA Ops:
  0.0 1.5 %copy.7.sizes = f32[256,1]{1,0:T(8,128)} copy(f32[256,1]{0,1:T(1,128)} %bitcast.1) | data formatting | bytes 2048 | tf_op jit(solution)/shard_map/reshape | solution.py:356
  1.5 133.7 %shard_map.64 = f32[9,16,4096]{2,1,0:T(8,128)} custom-call(s32[5]{0:T(128)} %offsets.1, f32[9,16,4096]{2,1,0:T(8,128)} %right.1, bf16[9,5,256,256]{3,2,1,0:T(8,128)(2,1)} %coupling.1, bf16[256,256]{1,0:T(8,128)(2,1)} %basis.1, bf16[256,256]{1,0:T(8,128)(2,1)} %inverse.1, f32[256,1]{1,0:T(8,128)} %copy.7.sizes), custom_call_target="tpu_custom_call" | custom-call | tf_op jit(solution)/shard_map/pallas_call | solution.py:320
  135.2 3.3 %copy.9 = f32[9,16,4096]{2,1,0:T(8,128)} copy(f32[9,16,4096]{2,1,0:T(8,128)} %shard_map.64) | data formatting | bytes 4718592

commit v2 on v1

--- a/solution.py
+++ b/solution.py
@@ -18,10 +18,9 @@
 COLS = KZ * R // NZ
 SPANS = KZ // NZ
 MESH = pl.DeviceIdType.MESH
-PARTS_OF = ((0,), (1, 2), (3,))
-
-CHUNK = 3
-CHUNKS = M // CHUNK
+PACE = ((15, 0, 0, 0, 0), (15, 0, 0, 0, 0))
+ORDER = (3, 4, 5, 0, 6, 1, 7, 2, 8)
+WINDOW = 4
 
 
 def flip(place):
@@ -77,19 +76,25 @@
     def rows(place):
         return pl.ds(pl.multiple_of(place * ROWS, ROWS), ROWS)
 
-    def modes(chunk):
-        return pl.ds(chunk * CHUNK, CHUNK)
-
-    def inward(chunk, k):
+    def inward(m, k):
         to = (sz + k) % NZ
         return pltpu.make_async_remote_copy(
-            src_ref=right.at[modes(chunk), :, columns(group_of(sx, to))],
-            dst_ref=start.at[modes(chunk), rows(sz), :],
-            send_sem=in_send.at[chunk, k],
-            recv_sem=in_recv.at[chunk, k],
+            src_ref=right.at[m, :, columns(group_of(sx, to))],
+            dst_ref=start.at[m, rows(sz), :],
+            send_sem=in_send.at[m],
+            recv_sem=in_recv.at[m],
             device_id=(sx, to),
             device_id_type=MESH,
         )
+
+    def send_mode(m):
+        @pl.loop(1, NZ)
+        def _(k):
+            inward(m, k).start()
+
+    def all_but_own(m, sem):
+        part = start.at[m, pl.ds(0, NC - ROWS), :]
+        return pltpu.make_async_copy(part, part, sem)
 
     def outward(step, k):
         to = (sz + k) % NZ
@@ -102,31 +107,48 @@
             device_id_type=MESH,
         )
 
+    def send_share(step, stage):
+        begin = 1 + sum(PACE[step][:stage])
+
+        @pl.loop(begin, begin + PACE[step][stage])
+        def _(k):
+            outward(step, k).start()
+
+    def send_one(step, stage, m):
+        begin = 1 + sum(PACE[step][:stage])
+
+        @pl.when(m < PACE[step][stage])
+        def _():
+            outward(step, begin + m).start()
+
     def halo(step, part):
-        to, begin, end = (
-            (down, 0, M), (down, 3, M + 3), (up, 3, -OFF + 0), (up, 6, -OFF + 3),
-        )[part]
-        return pltpu.make_async_remote_copy(
-            src_ref=search.at[step, pl.ds(OFF + begin, 3)],
-            dst_ref=search.at[step, pl.ds(OFF + end, 3)],
+        to, begin, end = (down, part, M + part) if part < OFF else (up, part - 3, part - 2 * OFF)
+        return pltpu.make_async_remote_copy(
+            src_ref=search.at[step, OFF + begin],
+            dst_ref=search.at[step, OFF + end],
             send_sem=halo_send.at[step, part],
             recv_sem=halo_recv.at[step, part],
             device_id=to,
             device_id_type=MESH,
         )
 
-    for chunk in range(CHUNKS):
-
-        @pl.loop(1, NZ)
-        def _(k):
-            inward(chunk, k).start()
+    def send_halo(step, m):
+        if m < OFF:
+            halo(step, m).start()
+        if m >= M - OFF:
+            halo(step, m + 3).start()
+
+    for m in ORDER[:WINDOW]:
+        send_mode(m)
 
     own = pltpu.make_async_copy(right.at[:, :, columns(group)], start.at[:, rows(sz), :], local_sem.at[0])
     own.start()
 
+    sizes_down = jnp.transpose(jnp.broadcast_to(sizes[...], (NC, NC)))
+
     @pl.loop(0, M)
     def _(m):
-        factor[m] = -1.0 / (sizes[...] + wave_row(sx, m, group))
+        factor[m] = -1.0 / (sizes_down + wave_row(sx, m, group))
 
     own.wait()
 
@@ -137,12 +159,14 @@
         search[step, OFF + m] = result.astype(jnp.bfloat16)
 
     def apply(step):
-        for part in range(4):
+        for part in range(2 * OFF):
             halo(step, part).wait_recv()
+
         sums[...] = jnp.zeros_like(sums)
 
         @pl.loop(0, M)
         def _(m):
+            send_one(step, 1, m)
             total = -wave_row(sx, m, group) * search[step, OFF + m].astype(jnp.float32)
             for h in range(H):
                 total = total + jnp.dot(
@@ -195,6 +219,8 @@
         def _(k):
             row_copy(step, k).start()
 
+        send_share(step, 2)
+
         @pl.loop(1, NZ)
         def _(k):
             row_copy(step, k).wait_recv()
@@ -208,6 +234,8 @@
         @pl.loop(1, NX)
         def _(k):
             all_copy(step, k).start()
+
+        send_share(step, 3)
 
         @pl.loop(1, NX)
         def _(k):
@@ -222,23 +250,14 @@
         energy = jnp.where(first_half, other, of_all)
         return (aligned / (energy + 1e-6))[0:1]
 
-    for chunk in range(CHUNKS):
-
-        @pl.loop(1, NZ)
-        def _(k):
-            inward(chunk, k).wait_recv()
-
-        @pl.loop(chunk * CHUNK, chunk * CHUNK + CHUNK)
-        def _(m):
-            precondition(0, m, start[m].astype(jnp.bfloat16))
-
-        for part in PARTS_OF[chunk]:
-            halo(0, part).start()
-
-    @pl.loop(1, NZ)
-    def _(k):
-        outward(0, k).start()
-
+    for place, m in enumerate(ORDER):
+        all_but_own(m, in_recv.at[m]).wait()
+        if place + WINDOW < M:
+            send_mode(ORDER[place + WINDOW])
+        precondition(0, m, start[m].astype(jnp.bfloat16))
+        send_halo(0, m)
+
+    send_share(0, 0)
     own_first = pltpu.make_async_copy(
         search.at[0, pl.ds(OFF, M), rows(sz), :], back.at[0, :, :, columns(group)], local_sem.at[1]
     )
@@ -250,21 +269,13 @@
     first = step_size(0)
     first_wide = jnp.concatenate([first, first], axis=1)
 
-    for chunk in range(CHUNKS):
-
-        @pl.loop(chunk * CHUNK, chunk * CHUNK + CHUNK)
-        def _(m):
-            left = start[m] - first_wide * image[m]
-            residual[m] = left
-            precondition(1, m, left.astype(jnp.bfloat16))
-
-        for part in PARTS_OF[chunk]:
-            halo(1, part).start()
-
-    @pl.loop(1, NZ)
-    def _(k):
-        outward(1, k).start()
-
+    for m in ORDER:
+        left = start[m] - first_wide * image[m]
+        residual[m] = left
+        precondition(1, m, left.astype(jnp.bfloat16))
+        send_halo(1, m)
+
+    send_share(1, 0)
     own_second = pltpu.make_async_copy(
         search.at[1, pl.ds(OFF, M), rows(sz), :], back.at[1, :, :, columns(group)], local_sem.at[2]
     )
@@ -291,8 +302,6 @@
 
     @pl.loop(1, NZ)
     def _(k):
-        for chunk in range(CHUNKS):
-            inward(chunk, k).wait_send()
         outward(0, k).wait_send()
         outward(1, k).wait_send()
         row_copy(0, k).wait_send()
@@ -303,8 +312,11 @@
         all_copy(0, k).wait_send()
         all_copy(1, k).wait_send()
 
+    for m in range(M):
+        all_but_own(m, in_send.at[m]).wait()
+
     for step in range(2):
-        for part in range(4):
+        for part in range(2 * OFF):
             halo(step, part).wait_send()
 
     @pl.loop(0, M)
@@ -337,12 +349,12 @@
             pltpu.VMEM((2, 1, 128), full),
             pltpu.VMEM((2, NX, 1, 128), full),
             dma((1,)),
-            dma((CHUNKS, NZ)),
-            dma((CHUNKS, NZ)),
+            dma((M,)),
+            dma((M,)),
             dma((2, NZ)),
             dma((2, NZ)),
-            dma((2, 4)),
-            dma((2, 4)),
+            dma((2, 2 * OFF)),
+            dma((2, 2 * OFF)),
             dma((2, NZ)),
             dma((2, NZ)),
             dma((2, NX)),
@@ -353,7 +365,7 @@
         compiler_params=pltpu.CompilerParams(
             collective_id=0, has_side_effects=True, vmem_limit_bytes=56 * 2**20
         ),
-    )(harmonic_offsets, right_side, coupling, eigen_basis, eigen_inverse, eigen_size.reshape(NC, 1))
+    )(harmonic_offsets, right_side, coupling, eigen_basis, eigen_inverse, eigen_size.reshape(1, NC))
 
 
 def solution(mesh):

time: 139 us -> 134 us (0.964)
  Pallas kernels: 134 us -> 130 us
  local copies, waits for them, and re-layouts: 4.75 us -> 3.27 us
    pallas_call x1, Pallas kernels: 134 us -> 130 us  [shards(): pl.pallas_call(kernel, out_shape=jax.ShapeDtypeStruct((M, ROWS, KZ * R),...]
    reshape x1 -> x0, local copies, waits for them, and re-layouts: 1.47 us -> none  [shards(): eigen_size.reshape(NC, 1)]
where the time goes in v2:
time: 134 us
  Pallas kernels  130 us (97%)
  local copies, waits for them, and re-layouts  3.27 us (2%)
    pallas_call x1, Pallas kernels, shards(): pl.pallas_call(kernel, out_shape=jax.ShapeDtypeStruct((M, ROWS, KZ * R),...  130 us
    unnamed x1, local copies, waits for them, and re-layouts  3.27 us

profile of v2, /device:TPU:1, one launch (start us, length us, event | category | flops | bytes accessed | tf_op | source)
XLA Modules:
  0.0 133.6 jit_solution(15916531583687212490)
XLA Ops:
  0.0 130.3 %shard_map.64 = f32[9,16,4096]{2,1,0:T(8,128)} custom-call(s32[5]{0:T(128)} %offsets.1, f32[9,16,4096]{2,1,0:T(8,128)} %right.1, bf16[9,5,256,256]{3,2,1,0:T(8,128)(2,1)} %coupling.1, bf16[256,256]{1,0:T(8,128)(2,1)} %basis.1, bf16[256,256]{1,0:T(8,128)(2,1)} %inverse.1, f32[1,256]{1,0:T(1,128)} %bitcast.1), custom_call_target="tpu_custom_call" | custom-call | tf_op jit(solution)/shard_map/pallas_call | solution.py:332
  130.4 3.3 %copy.8 = f32[9,16,4096]{2,1,0:T(8,128)} copy(f32[9,16,4096]{2,1,0:T(8,128)} %shard_map.64) | data formatting | bytes 4718592

commit v3 on v2

v3 whole, which is shorter than its diff:
```python
import jax
import jax.numpy as jnp
from jax import lax
from jax.experimental import pallas as pl
from jax.experimental.pallas import tpu as pltpu
from jax.sharding import PartitionSpec as P

KX = 72
KZ = 128
NC = 256
H = 5
OFF = 6
R = 32
NX = 8
NZ = 16
M = KX // NX
ROWS = NC // NZ
COLS = KZ * R // NZ
SPANS = KZ // NZ
QUARTER = NC // 4
MESH = pl.DeviceIdType.MESH
WINDOW = 4
PACE = ((15, 0, 0, 0, 0), (15, 0, 0, 0, 0))


def device_at(x, y, z, core):
    return 2 * y + z % 2, 4 * x + 2 * (z // 2) + core


def wave_row(block, mode, group):
    index = block * M + mode
    signed_x = jnp.where(index < KX // 2, index, index - KX).astype(jnp.float32) * (4.0 / KX)
    column = lax.broadcasted_iota(jnp.int32, (1, COLS), 1)
    span = group * SPANS + column // R
    signed_z = jnp.where(span < KZ // 2, span, span - KZ).astype(jnp.float32) * (4.0 / KZ)
    return 1.0 + signed_x * signed_x + signed_z * signed_z


def kernel(
    offsets, right, coupling, basis, inverse, sizes, out,
    start, factor, image, residual, blocks,
    search, back, final, sums, parts, row_sums, row_total, all_sums,
    load_sem, in_send, in_near, in_recv, out_send, out_near, out_recv, halo_send, halo_recv,
    block_send, block_recv, pass_send, row_send, row_recv, all_send, all_recv, final_sem,
):
    sx, sz = lax.axis_index("sx"), lax.axis_index("sz")
    y, low_z = sx // 2, sx % 2
    x, core = sz // 4, sz % 2
    z = 2 * ((sz // 2) % 2) + low_z
    block = 2 * y + core
    group = 4 * x + z
    at_home = core == low_z
    away = core != low_z
    other = sz + 1 - 2 * core
    up = ((sx + 2 * core) % NX, other)
    down = ((sx + NX - 2 * (1 - core)) % NX, other)
    across = ((sx + NX + 4 * core - 2) % NX, other)

    load_blocks = pltpu.make_async_copy(coupling, blocks, load_sem.at[0])

    @pl.when(at_home)
    def _():
        load_blocks.start()

    barrier = pltpu.get_barrier_semaphore()

    place = NZ * low_z + sz

    @pl.loop(1, 2 * NZ)
    def _(k):
        to = (place + k) % (2 * NZ)
        pl.semaphore_signal(barrier, inc=1, device_id=(2 * y + to // NZ, to % NZ), device_id_type=MESH)

    @pl.loop(1, NX)
    def _(k):
        pl.semaphore_signal(barrier, inc=1, device_id=((sx + k) % NX, sz), device_id_type=MESH)

    pl.semaphore_signal(barrier, inc=1, device_id=across, device_id_type=MESH)
    pl.semaphore_wait(barrier, 2 * NZ - 1 + NX - 1 + 1)

    def columns(index):
        return pl.ds(pl.multiple_of(index * COLS, COLS), COLS)

    def rows(index):
        return pl.ds(pl.multiple_of(index * ROWS, ROWS), ROWS)

    def quarter(index):
        return pl.ds(pl.multiple_of(index * QUARTER, QUARTER), QUARTER)

    def push(side):
        index = 2 * (x % 2) + side
        return pltpu.make_async_remote_copy(
            src_ref=coupling.at[:, :, quarter(index), :],
            dst_ref=blocks.at[:, :, quarter(index), :],
            send_sem=block_send.at[side],
            recv_sem=block_recv.at[index],
            device_id=device_at(x, y, (z + 1 + 2 * side) % 4, core),
            device_id_type=MESH,
        )

    def forward(side):
        index = 2 * (x % 2) + side
        return pltpu.make_async_remote_copy(
            src_ref=blocks.at[:, :, quarter(index), :],
            dst_ref=blocks.at[:, :, quarter(index), :],
            send_sem=pass_send.at[side],
            recv_sem=block_recv.at[index],
            device_id=(sx, (sz + 4 + 8 * side) % NZ),
            device_id_type=MESH,
        )

    def arrived(index):
        part = blocks.at[:, :, quarter(index), :]
        return pltpu.make_async_copy(part, part, block_recv.at[index])

    @pl.when(at_home)
    def _():
        for side in range(2):
            push(side).start()

    def inward(m, k, send_sem):
        to = (group + k) % NZ
        return pltpu.make_async_remote_copy(
            src_ref=right.at[m, :, columns(to)],
            dst_ref=start.at[m, rows(sz), :],
            send_sem=send_sem,
            recv_sem=in_recv.at[m],
            device_id=device_at(to // 4, y, to % 4, low_z),
            device_id_type=MESH,
        )

    def send_mode(m):
        @pl.when(at_home)
        def _():
            pltpu.make_async_copy(right.at[m, :, columns(group)], start.at[m, rows(sz), :], in_recv.at[m]).start()

        @pl.when(away)
        def _():
            inward(m, 0, in_near.at[m]).start()

        @pl.loop(1, NZ)
        def _(k):
            inward(m, k, in_send.at[m]).start()

    def outward(step, k, send_sem):
        to = (sz + k) % NZ
        return pltpu.make_async_remote_copy(
            src_ref=search.at[step, pl.ds(OFF, M), rows(to), :],
            dst_ref=back.at[step, :, :, columns(group)],
            send_sem=send_sem,
            recv_sem=out_recv.at[step],
            device_id=(block, to),
            device_id_type=MESH,
        )

    def send_near(step):
        @pl.when(at_home)
        def _():
            pltpu.make_async_copy(
                search.at[step, pl.ds(OFF, M), rows(sz), :], back.at[step, :, :, columns(group)], out_recv.at[step]
            ).start()

        @pl.when(away)
        def _():
            outward(step, 0, out_near.at[step]).start()

    def send_share(step, stage):
        begin = 1 + sum(PACE[step][:stage])

        @pl.loop(begin, begin + PACE[step][stage])
        def _(k):
            outward(step, k, out_send.at[step]).start()

    def send_one(step, stage, m):
        begin = 1 + sum(PACE[step][:stage])

        @pl.when(m < PACE[step][stage])
        def _():
            outward(step, begin + m, out_send.at[step]).start()

    def halo_down(step, m):
        return pltpu.make_async_remote_copy(
            src_ref=search.at[step, OFF + m],
            dst_ref=search.at[step, OFF + M + m],
            send_sem=halo_send.at[step, m],
            recv_sem=halo_recv.at[step, m],
            device_id=down,
            device_id_type=MESH,
        )

    def halo_up(step, m):
        return pltpu.make_async_remote_copy(
            src_ref=search.at[step, OFF + m],
            dst_ref=search.at[step, m - (M - OFF)],
            send_sem=halo_send.at[step, m + M - OFF],
            recv_sem=halo_recv.at[step, m + M - OFF],
            device_id=up,
            device_id_type=MESH,
        )

    def send_halo(step, m):
        @pl.when(m < OFF)
        def _():
            halo_down(step, m).start()

        @pl.when(m >= M - OFF)
        def _():
            halo_up(step, m).start()

    for m in range(WINDOW):
        send_mode((m + 3) % M)

    sizes_down = jnp.transpose(jnp.broadcast_to(sizes[...], (NC, NC)))

    @pl.loop(0, M)
    def _(m):
        factor[m] = -1.0 / (sizes_down + wave_row(block, m, group))

    def precondition(step, m, rounded):
        spectral = jnp.dot(inverse[...], rounded, preferred_element_type=jnp.float32)
        scaled = (spectral * factor[m]).astype(jnp.bfloat16)
        result = jnp.dot(basis[...], scaled, preferred_element_type=jnp.float32)
        search[step, OFF + m] = result.astype(jnp.bfloat16)

    def apply(step):
        @pl.loop(0, OFF)
        def _(m):
            halo_down(step, m).wait_recv()
            halo_up(step, m + M - OFF).wait_recv()

        sums[...] = jnp.zeros_like(sums)

        @pl.loop(0, M)
        def _(m):
            send_one(step, 1, m)
            total = -wave_row(block, m, group) * search[step, OFF + m].astype(jnp.float32)
            for h in range(H):
                total = total + jnp.dot(
                    blocks[m, h], search[step, OFF + m + offsets[h]], preferred_element_type=jnp.float32
                )
            if step == 0:
                image[m] = total
                before = start[m]
            else:
                before = residual[m]
            sums[0] += jnp.sum((total * before).reshape(NC // 8, 8, COLS), axis=0)
            sums[1] += jnp.sum((total * total).reshape(NC // 8, 8, COLS), axis=0)

    def row_copy(step, k):
        to = (sz + k) % NZ
        return pltpu.make_async_remote_copy(
            src_ref=parts.at[step],
            dst_ref=row_sums.at[step, sz],
            send_sem=row_send.at[step, k],
            recv_sem=row_recv.at[step, k],
            device_id=(sx, to),
            device_id_type=MESH,
        )

    def all_copy(step, k):
        to = (sx + k) % NX
        return pltpu.make_async_remote_copy(
            src_ref=row_total.at[step],
            dst_ref=all_sums.at[step, sx],
            send_sem=all_send.at[step, k],
            recv_sem=all_recv.at[step, k],
            device_id=(to, sz),
            device_id_type=MESH,
        )

    first_half = lax.broadcasted_iota(jnp.int32, (8, 128), 1) < 64

    def step_size(step):
        def fold(value):
            value = value[:, :128] + value[:, 128:]
            value = value + pltpu.roll(value, 64, 1)
            return value + pltpu.roll(value, 32, 1)

        both = jnp.where(first_half, fold(sums[0]), fold(sums[1]))
        mine = jnp.sum(both, axis=0, keepdims=True)
        parts[step] = mine
        row_sums[step, sz] = mine

        @pl.loop(1, NZ)
        def _(k):
            row_copy(step, k).start()

        send_share(step, 2)

        @pl.loop(1, NZ)
        def _(k):
            row_copy(step, k).wait_recv()

        of_row = row_sums[step, 0]
        for index in range(1, NZ):
            of_row = of_row + row_sums[step, index]
        row_total[step] = of_row
        all_sums[step, sx] = of_row

        @pl.loop(1, NX)
        def _(k):
            all_copy(step, k).start()

        send_share(step, 3)

        @pl.loop(1, NX)
        def _(k):
            all_copy(step, k).wait_recv()

        of_all = all_sums[step, 0]
        for index in range(1, NX):
            of_all = of_all + all_sums[step, index]
        of_all = jnp.broadcast_to(of_all, (8, 128))
        swapped = pltpu.roll(of_all, 64, 1)
        aligned = jnp.where(first_half, of_all, swapped)
        energy = jnp.where(first_half, swapped, of_all)
        return (aligned / (energy + 1e-6))[0:1]

    def first_modes(begin, end):
        @pl.loop(begin, end)
        def _(turn):
            m = (turn + 3) % M
            pltpu.make_async_copy(start.at[m], start.at[m], in_recv.at[m]).wait()

            @pl.when(turn + WINDOW < M)
            def _():
                send_mode((turn + WINDOW + 3) % M)

            precondition(0, m, start[m].astype(jnp.bfloat16))
            send_halo(0, m)

    first_modes(0, PASS_AFTER)

    @pl.when(away)
    def _():
        for side in range(2):
            arrived(2 * (x % 2) + side).wait()
            forward(side).start()

    first_modes(PASS_AFTER, M)
    send_near(0)
    send_share(0, 0)

    @pl.when(at_home)
    def _():
        load_blocks.wait()

    @pl.when(away)
    def _():
        for side in range(2):
            arrived(2 * (1 - x % 2) + side).wait()

    apply(0)
    first = step_size(0)
    first_wide = jnp.concatenate([first, first], axis=1)

    @pl.loop(0, M)
    def _(turn):
        m = (turn + 3) % M
        send_one(0, 4, turn)
        left = start[m] - first_wide * image[m]
        residual[m] = left
        precondition(1, m, left.astype(jnp.bfloat16))
        send_halo(1, m)

    send_near(1)
    send_share(1, 0)
    apply(1)
    second = step_size(1)

    for step in range(2):
        pltpu.make_async_copy(back.at[step], back.at[step], out_recv.at[step]).wait()

    reach = KZ * R // 128
    first_all = jnp.tile(first, (1, reach))
    second_all = jnp.tile(second, (1, reach))

    @pl.loop(0, M)
    def _(m):
        final[m] = first_all * back[0, m].astype(jnp.float32) + second_all * back[1, m].astype(jnp.float32)
        pltpu.make_async_copy(final.at[m], out.at[m], final_sem.at[m]).start()

    @pl.loop(0, M)
    def _(m):
        part = start.at[m, pl.ds(0, NC - ROWS), :]
        pltpu.make_async_copy(part, part, in_send.at[m]).wait()

    for step in range(2):
        part = search.at[step, pl.ds(OFF, M), pl.ds(0, NC - ROWS), :]
        pltpu.make_async_copy(part, part, out_send.at[step]).wait()

    @pl.when(at_home)
    def _():
        for side in range(2):
            push(side).wait_send()

    @pl.when(away)
    def _():
        @pl.loop(0, M)
        def _(m):
            inward(m, 0, in_near.at[m]).wait_send()

        for step in range(2):
            outward(step, 0, out_near.at[step]).wait_send()
        for side in range(2):
            forward(side).wait_send()

    for step in range(2):

        @pl.loop(1, NZ)
        def _(k):
            row_copy(step, k).wait_send()

        @pl.loop(1, NX)
        def _(k):
            all_copy(step, k).wait_send()

        @pl.loop(0, OFF)
        def _(m):
            halo_down(step, m).wait_send()
            halo_up(step, m + M - OFF).wait_send()

    @pl.loop(0, M)
    def _(m):
        pltpu.make_async_copy(final.at[m], out.at[m], final_sem.at[m]).wait()


PASS_AFTER = 5


def shards(right_side, coupling, harmonic_offsets, eigen_basis, eigen_inverse, eigen_size):
    vmem = pl.BlockSpec(memory_space=pltpu.VMEM)
    anywhere = pl.BlockSpec(memory_space=pl.ANY)
    low, full = jnp.bfloat16, jnp.float32
    dma = pltpu.SemaphoreType.DMA
    return pl.pallas_call(
        kernel,
        out_shape=jax.ShapeDtypeStruct((M, ROWS, KZ * R), full),
        in_specs=[pl.BlockSpec(memory_space=pltpu.SMEM), anywhere, anywhere, vmem, vmem, vmem],
        out_specs=anywhere,
        scratch_shapes=[
            pltpu.VMEM((M, NC, COLS), full),
            pltpu.VMEM((M, NC, COLS), full),
            pltpu.VMEM((M, NC, COLS), full),
            pltpu.VMEM((M, NC, COLS), full),
            pltpu.VMEM((M, H, NC, NC), low),
            pltpu.VMEM((2, M + 2 * OFF, NC, COLS), low),
            pltpu.VMEM((2, M, ROWS, KZ * R), low),
            pltpu.VMEM((M, ROWS, KZ * R), full),
            pltpu.VMEM((2, 8, COLS), full),
            pltpu.VMEM((2, 1, 128), full),
            pltpu.VMEM((2, NZ, 1, 128), full),
            pltpu.VMEM((2, 1, 128), full),
            pltpu.VMEM((2, NX, 1, 128), full),
            dma((1,)),
            dma((M,)),
            dma((M,)),
            dma((M,)),
            dma((2,)),
            dma((2,)),
            dma((2,)),
            dma((2, 2 * OFF)),
            dma((2, 2 * OFF)),
            dma((2,)),
            dma((4,)),
            dma((2,)),
            dma((2, NZ)),
            dma((2, NZ)),
            dma((2, NX)),
            dma((2, NX)),
            dma((M,)),
        ],
        compiler_params=pltpu.CompilerParams(
            collective_id=0, has_side_effects=True, vmem_limit_bytes=56 * 2**20
        ),
    )(harmonic_offsets, right_side, coupling, eigen_basis, eigen_inverse, eigen_size.reshape(1, NC))


def solution(mesh):
    in_specs = (P("sx", "sz", None), P("sx", None, None, None), P(), P(), P(), P())
    out_specs = P("sx", "sz", None)
    return jax.shard_map(shards, mesh=mesh, in_specs=in_specs, out_specs=out_specs, check_vma=False)
```

time: 134 us -> 123 us (0.918)
  Pallas kernels: 130 us -> 119 us
    pallas_call x1, Pallas kernels: 130 us -> 119 us  [shards(): pl.pallas_call(kernel, out_shape=jax.ShapeDtypeStruct((M, ROWS, KZ * R),...]
where the time goes in v3:
time: 123 us
  Pallas kernels  119 us (97%)
  local copies, waits for them, and re-layouts  3.27 us (3%)
    pallas_call x1, Pallas kernels, shards(): pl.pallas_call(kernel, out_shape=jax.ShapeDtypeStruct((M, ROWS, KZ * R),...  119 us
    unnamed x1, local copies, waits for them, and re-layouts  3.27 us

profile of v3, /device:TPU:1, one launch (start us, length us, event | category | flops | bytes accessed | tf_op | source)
XLA Modules:
  0.0 122.6 jit_solution(1202953103912072223)
XLA Ops:
  0.0 119.4 %shard_map.64 = f32[9,16,4096]{2,1,0:T(8,128)} custom-call(s32[5]{0:T(128)} %offsets.1, f32[9,16,4096]{2,1,0:T(8,128)} %right.1, bf16[9,5,256,256]{3,2,1,0:T(8,128)(2,1)} %coupling.1, bf16[256,256]{1,0:T(8,128)(2,1)} %basis.1, bf16[256,256]{1,0:T(8,128)(2,1)} %inverse.1, f32[1,256]{1,0:T(1,128)} %bitcast.1), custom_call_target="tpu_custom_call" | custom-call | tf_op jit(solution)/shard_map/pallas_call | solution.py:436
  119.4 3.3 %copy.8 = f32[9,16,4096]{2,1,0:T(8,128)} copy(f32[9,16,4096]{2,1,0:T(8,128)} %shard_map.64) | data formatting | bytes 4718592

commit v4 on v3

--- a/solution.py
+++ b/solution.py
@@ -20,7 +20,8 @@
 QUARTER = NC // 4
 MESH = pl.DeviceIdType.MESH
 WINDOW = 4
-PACE = ((15, 0, 0, 0, 0), (15, 0, 0, 0, 0))
+LAG = 1
+PACE = ((0, 2, 4, 4, 5), (8, 0, 4, 3, 0))
 
 
 def device_at(x, y, z, core):
@@ -87,36 +88,38 @@
     def quarter(index):
         return pl.ds(pl.multiple_of(index * QUARTER, QUARTER), QUARTER)
 
-    def push(side):
+    def push(m, side):
         index = 2 * (x % 2) + side
         return pltpu.make_async_remote_copy(
-            src_ref=coupling.at[:, :, quarter(index), :],
-            dst_ref=blocks.at[:, :, quarter(index), :],
-            send_sem=block_send.at[side],
-            recv_sem=block_recv.at[index],
+            src_ref=coupling.at[m, :, quarter(index), :],
+            dst_ref=blocks.at[m, :, quarter(index), :],
+            send_sem=block_send.at[m, side],
+            recv_sem=block_recv.at[m, index],
             device_id=device_at(x, y, (z + 1 + 2 * side) % 4, core),
             device_id_type=MESH,
         )
 
-    def forward(side):
+    def forward(m, side):
         index = 2 * (x % 2) + side
         return pltpu.make_async_remote_copy(
-            src_ref=blocks.at[:, :, quarter(index), :],
-            dst_ref=blocks.at[:, :, quarter(index), :],
-            send_sem=pass_send.at[side],
-            recv_sem=block_recv.at[index],
+            src_ref=blocks.at[m, :, quarter(index), :],
+            dst_ref=blocks.at[m, :, quarter(index), :],
+            send_sem=pass_send.at[m, side],
+            recv_sem=block_recv.at[m, index],
             device_id=(sx, (sz + 4 + 8 * side) % NZ),
             device_id_type=MESH,
         )
 
-    def arrived(index):
-        part = blocks.at[:, :, quarter(index), :]
-        return pltpu.make_async_copy(part, part, block_recv.at[index])
-
-    @pl.when(at_home)
-    def _():
-        for side in range(2):
-            push(side).start()
+    def arrived(m, index):
+        part = blocks.at[m, :, quarter(index), :]
+        return pltpu.make_async_copy(part, part, block_recv.at[m, index])
+
+    def pass_on(m):
+        @pl.when(away)
+        def _():
+            for side in range(2):
+                arrived(m, 2 * (x % 2) + side).wait()
+                forward(m, side).start()
 
     def inward(m, k, send_sem):
         to = (group + k) % NZ
@@ -129,9 +132,14 @@
             device_id_type=MESH,
         )
 
-    def send_mode(m):
+    def send_mode(turn):
+        m = (turn + 3) % M
+
         @pl.when(at_home)
         def _():
+            for side in range(2):
+                push(turn, side).start()
+
             pltpu.make_async_copy(right.at[m, :, columns(group)], start.at[m, rows(sz), :], in_recv.at[m]).start()
 
         @pl.when(away)
@@ -208,7 +216,7 @@
             halo_up(step, m).start()
 
     for m in range(WINDOW):
-        send_mode((m + 3) % M)
+        send_mode(m)
 
     sizes_down = jnp.transpose(jnp.broadcast_to(sizes[...], (NC, NC)))
 
@@ -232,6 +240,13 @@
 
         @pl.loop(0, M)
         def _(m):
+            if step == 0:
+
+                @pl.when(away)
+                def _():
+                    for side in range(2):
+                        arrived(m, 2 * (1 - x % 2) + side).wait()
+
             send_one(step, 1, m)
             total = -wave_row(block, m, group) * search[step, OFF + m].astype(jnp.float32)
             for h in range(H):
@@ -251,8 +266,8 @@
         return pltpu.make_async_remote_copy(
             src_ref=parts.at[step],
             dst_ref=row_sums.at[step, sz],
-            send_sem=row_send.at[step, k],
-            recv_sem=row_recv.at[step, k],
+            send_sem=row_send.at[step],
+            recv_sem=row_recv.at[step],
             device_id=(sx, to),
             device_id_type=MESH,
         )
@@ -262,8 +277,8 @@
         return pltpu.make_async_remote_copy(
             src_ref=row_total.at[step],
             dst_ref=all_sums.at[step, sx],
-            send_sem=all_send.at[step, k],
-            recv_sem=all_recv.at[step, k],
+            send_sem=all_send.at[step],
+            recv_sem=all_recv.at[step],
             device_id=(to, sz),
             device_id_type=MESH,
         )
@@ -287,9 +302,8 @@
 
         send_share(step, 2)
 
-        @pl.loop(1, NZ)
-        def _(k):
-            row_copy(step, k).wait_recv()
+        others = row_sums.at[step, pl.ds(0, NZ - 1)]
+        pltpu.make_async_copy(others, others, row_recv.at[step]).wait()
 
         of_row = row_sums[step, 0]
         for index in range(1, NZ):
@@ -303,9 +317,8 @@
 
         send_share(step, 3)
 
-        @pl.loop(1, NX)
-        def _(k):
-            all_copy(step, k).wait_recv()
+        others = all_sums.at[step, pl.ds(0, NX - 1)]
+        pltpu.make_async_copy(others, others, all_recv.at[step]).wait()
 
         of_all = all_sums[step, 0]
         for index in range(1, NX):
@@ -324,20 +337,21 @@
 
             @pl.when(turn + WINDOW < M)
             def _():
-                send_mode((turn + WINDOW + 3) % M)
+                send_mode(turn + WINDOW)
 
             precondition(0, m, start[m].astype(jnp.bfloat16))
             send_halo(0, m)
 
-    first_modes(0, PASS_AFTER)
-
-    @pl.when(away)
-    def _():
-        for side in range(2):
-            arrived(2 * (x % 2) + side).wait()
-            forward(side).start()
-
-    first_modes(PASS_AFTER, M)
+            @pl.when(turn >= LAG)
+            def _():
+                pass_on(turn - LAG)
+
+    first_modes(0, M)
+
+    @pl.loop(M - LAG, M)
+    def _(m):
+        pass_on(m)
+
     send_near(0)
     send_share(0, 0)
 
@@ -345,23 +359,26 @@
     def _():
         load_blocks.wait()
 
-    @pl.when(away)
-    def _():
-        for side in range(2):
-            arrived(2 * (1 - x % 2) + side).wait()
-
     apply(0)
     first = step_size(0)
     first_wide = jnp.concatenate([first, first], axis=1)
 
-    @pl.loop(0, M)
+    @pl.loop(0, M // 3)
     def _(turn):
-        m = (turn + 3) % M
-        send_one(0, 4, turn)
-        left = start[m] - first_wide * image[m]
-        residual[m] = left
-        precondition(1, m, left.astype(jnp.bfloat16))
-        send_halo(1, m)
+        modes = [(3 * turn + 3 + each) % M for each in range(3)]
+        rounded = []
+        for m in modes:
+            left = start[m] - first_wide * image[m]
+            residual[m] = left
+            rounded.append(left.astype(jnp.bfloat16))
+        spectral = [jnp.dot(inverse[...], each, preferred_element_type=jnp.float32) for each in rounded]
+        scaled = [(each * factor[m]).astype(jnp.bfloat16) for each, m in zip(spectral, modes)]
+        for each, m in zip(scaled, modes):
+            result = jnp.dot(basis[...], each, preferred_element_type=jnp.float32)
+            search[1, OFF + m] = result.astype(jnp.bfloat16)
+        for each, m in enumerate(modes):
+            send_halo(1, m)
+            send_one(0, 4, 3 * turn + each)
 
     send_near(1)
     send_share(1, 0)
@@ -391,29 +408,28 @@
 
     @pl.when(at_home)
     def _():
-        for side in range(2):
-            push(side).wait_send()
+        @pl.loop(0, M)
+        def _(m):
+            for side in range(2):
+                push(m, side).wait_send()
 
     @pl.when(away)
     def _():
         @pl.loop(0, M)
         def _(m):
             inward(m, 0, in_near.at[m]).wait_send()
+            for side in range(2):
+                forward(m, side).wait_send()
 
         for step in range(2):
             outward(step, 0, out_near.at[step]).wait_send()
-        for side in range(2):
-            forward(side).wait_send()
 
     for step in range(2):
 
-        @pl.loop(1, NZ)
-        def _(k):
-            row_copy(step, k).wait_send()
-
-        @pl.loop(1, NX)
-        def _(k):
-            all_copy(step, k).wait_send()
+        others = row_sums.at[step, pl.ds(0, NZ - 1)]
+        pltpu.make_async_copy(others, others, row_send.at[step]).wait()
+        others = all_sums.at[step, pl.ds(0, NX - 1)]
+        pltpu.make_async_copy(others, others, all_send.at[step]).wait()
 
         @pl.loop(0, OFF)
         def _(m):
@@ -423,9 +439,6 @@
     @pl.loop(0, M)
     def _(m):
         pltpu.make_async_copy(final.at[m], out.at[m], final_sem.at[m]).wait()
-
-
-PASS_AFTER = 5
 
 
 def shards(right_side, coupling, harmonic_offsets, eigen_basis, eigen_inverse, eigen_size):
@@ -461,13 +474,13 @@
             dma((2,)),
             dma((2, 2 * OFF)),
             dma((2, 2 * OFF)),
-            dma((2,)),
-            dma((4,)),
-            dma((2,)),
-            dma((2, NZ)),
-            dma((2, NZ)),
-            dma((2, NX)),
-            dma((2, NX)),
+            dma((M, 2)),
+            dma((M, 4)),
+            dma((M, 2)),
+            dma((2,)),
+            dma((2,)),
+            dma((2,)),
+            dma((2,)),
             dma((M,)),
         ],
         compiler_params=pltpu.CompilerParams(

time: 123 us -> 102 us (0.83)
  Pallas kernels: 119 us -> 98.9 us
    pallas_call x1, Pallas kernels: 119 us -> 98.9 us  [shards(): pl.pallas_call(kernel, out_shape=jax.ShapeDtypeStruct((M, ROWS, KZ * R),...]
where the time goes in v4:
time: 102 us
  Pallas kernels  98.9 us (97%)
  local copies, waits for them, and re-layouts  3.27 us (3%)
    pallas_call x1, Pallas kernels, shards(): pl.pallas_call(kernel, out_shape=jax.ShapeDtypeStruct((M, ROWS, KZ * R),...  98.9 us
    unnamed x1, local copies, waits for them, and re-layouts  3.27 us

profile of v4, /device:TPU:1, one launch (start us, length us, event | category | flops | bytes accessed | tf_op | source)
XLA Modules:
  0.0 102.1 jit_solution(10479825605307158572)
XLA Ops:
  0.0 98.9 %shard_map.64 = f32[9,16,4096]{2,1,0:T(8,128)} custom-call(s32[5]{0:T(128)} %offsets.1, f32[9,16,4096]{2,1,0:T(8,128)} %right.1, bf16[9,5,256,256]{3,2,1,0:T(8,128)(2,1)} %coupling.1, bf16[256,256]{1,0:T(8,128)(2,1)} %basis.1, bf16[256,256]{1,0:T(8,128)(2,1)} %inverse.1, f32[1,256]{1,0:T(1,128)} %bitcast.1), custom_call_target="tpu_custom_call" | custom-call | tf_op jit(solution)/shard_map/pallas_call | solution.py:449
  98.9 3.3 %copy.8 = f32[9,16,4096]{2,1,0:T(8,128)} copy(f32[9,16,4096]{2,1,0:T(8,128)} %shard_map.64) | data formatting | bytes 4718592

commit v5 on v4

--- a/solution.py
+++ b/solution.py
@@ -20,7 +20,8 @@
 QUARTER = NC // 4
 MESH = pl.DeviceIdType.MESH
 WINDOW = 4
-LAG = 1
+LATE = 0
+LAG = 0
 PACE = ((0, 2, 4, 4, 5), (8, 0, 4, 3, 0))
 
 
@@ -38,11 +39,11 @@
 
 
 def kernel(
-    offsets, right, coupling, basis, inverse, sizes, out,
+    offsets, right, coupling, basis, inverse, sizes, back, steps,
     start, factor, image, residual, blocks,
-    search, back, final, sums, parts, row_sums, row_total, all_sums,
+    search, sums, parts, row_sums, row_total, all_sums,
     load_sem, in_send, in_near, in_recv, out_send, out_near, out_recv, halo_send, halo_recv,
-    block_send, block_recv, pass_send, row_send, row_recv, all_send, all_recv, final_sem,
+    block_send, block_recv, pass_send, row_send, row_recv, all_send, all_recv,
 ):
     sx, sz = lax.axis_index("sx"), lax.axis_index("sz")
     y, low_z = sx // 2, sx % 2
@@ -137,9 +138,6 @@
 
         @pl.when(at_home)
         def _():
-            for side in range(2):
-                push(turn, side).start()
-
             pltpu.make_async_copy(right.at[m, :, columns(group)], start.at[m, rows(sz), :], in_recv.at[m]).start()
 
         @pl.when(away)
@@ -149,6 +147,11 @@
         @pl.loop(1, NZ)
         def _(k):
             inward(m, k, in_send.at[m]).start()
+
+        @pl.when(at_home & (turn >= LATE))
+        def _():
+            for side in range(2):
+                push(turn - LATE, side).start()
 
     def outward(step, k, send_sem):
         to = (sz + k) % NZ
@@ -238,16 +241,7 @@
 
         sums[...] = jnp.zeros_like(sums)
 
-        @pl.loop(0, M)
-        def _(m):
-            if step == 0:
-
-                @pl.when(away)
-                def _():
-                    for side in range(2):
-                        arrived(m, 2 * (1 - x % 2) + side).wait()
-
-            send_one(step, 1, m)
+        def one(m):
             total = -wave_row(block, m, group) * search[step, OFF + m].astype(jnp.float32)
             for h in range(H):
                 total = total + jnp.dot(
@@ -260,6 +254,22 @@
                 before = residual[m]
             sums[0] += jnp.sum((total * before).reshape(NC // 8, 8, COLS), axis=0)
             sums[1] += jnp.sum((total * total).reshape(NC // 8, 8, COLS), axis=0)
+
+        @pl.loop(0, M // 3)
+        def _(turn):
+            modes = [3 * turn + each for each in range(3)]
+            if step == 0:
+
+                @pl.when(away)
+                def _():
+                    for m in modes:
+                        for side in range(2):
+                            arrived(m, 2 * (1 - x % 2) + side).wait()
+
+            for m in modes:
+                send_one(step, 1, m)
+            for m in modes:
+                one(m)
 
     def row_copy(step, k):
         to = (sz + k) % NZ
@@ -388,14 +398,8 @@
     for step in range(2):
         pltpu.make_async_copy(back.at[step], back.at[step], out_recv.at[step]).wait()
 
-    reach = KZ * R // 128
-    first_all = jnp.tile(first, (1, reach))
-    second_all = jnp.tile(second, (1, reach))
-
-    @pl.loop(0, M)
-    def _(m):
-        final[m] = first_all * back[0, m].astype(jnp.float32) + second_all * back[1, m].astype(jnp.float32)
-        pltpu.make_async_copy(final.at[m], out.at[m], final_sem.at[m]).start()
+    steps[0:1, :] = first
+    steps[1:2, :] = second
 
     @pl.loop(0, M)
     def _(m):
@@ -436,9 +440,31 @@
             halo_down(step, m).wait_send()
             halo_up(step, m + M - OFF).wait_send()
 
+
+def combine(steps, back, out, first, second, total, in_sem, out_sem):
+    def fetch(m, step, into):
+        return pltpu.make_async_copy(back.at[step, m], into.at[m], in_sem.at[step, m])
+
+    def store(m):
+        return pltpu.make_async_copy(total.at[m], out.at[m], out_sem.at[m])
+
     @pl.loop(0, M)
     def _(m):
-        pltpu.make_async_copy(final.at[m], out.at[m], final_sem.at[m]).wait()
+        fetch(m, 0, first).start()
+        fetch(m, 1, second).start()
+
+    wide = jnp.tile(steps[...], (1, KZ * R // 128))
+
+    @pl.loop(0, M)
+    def _(m):
+        fetch(m, 0, first).wait()
+        fetch(m, 1, second).wait()
+        total[m] = wide[0:1] * first[m].astype(jnp.float32) + wide[1:2] * second[m].astype(jnp.float32)
+        store(m).start()
+
+    @pl.loop(0, M)
+    def _(m):
+        store(m).wait()
 
 
 def shards(right_side, coupling, harmonic_offsets, eigen_basis, eigen_inverse, eigen_size):
@@ -446,11 +472,11 @@
     anywhere = pl.BlockSpec(memory_space=pl.ANY)
     low, full = jnp.bfloat16, jnp.float32
     dma = pltpu.SemaphoreType.DMA
-    return pl.pallas_call(
+    back, steps = pl.pallas_call(
         kernel,
-        out_shape=jax.ShapeDtypeStruct((M, ROWS, KZ * R), full),
+        out_shape=(jax.ShapeDtypeStruct((2, M, ROWS, KZ * R), low), jax.ShapeDtypeStruct((2, 128), full)),
         in_specs=[pl.BlockSpec(memory_space=pltpu.SMEM), anywhere, anywhere, vmem, vmem, vmem],
-        out_specs=anywhere,
+        out_specs=(anywhere, vmem),
         scratch_shapes=[
             pltpu.VMEM((M, NC, COLS), full),
             pltpu.VMEM((M, NC, COLS), full),
@@ -458,8 +484,6 @@
             pltpu.VMEM((M, NC, COLS), full),
             pltpu.VMEM((M, H, NC, NC), low),
             pltpu.VMEM((2, M + 2 * OFF, NC, COLS), low),
-            pltpu.VMEM((2, M, ROWS, KZ * R), low),
-            pltpu.VMEM((M, ROWS, KZ * R), full),
             pltpu.VMEM((2, 8, COLS), full),
             pltpu.VMEM((2, 1, 128), full),
             pltpu.VMEM((2, NZ, 1, 128), full),
@@ -481,12 +505,24 @@
             dma((2,)),
             dma((2,)),
             dma((2,)),
-            dma((M,)),
         ],
         compiler_params=pltpu.CompilerParams(
             collective_id=0, has_side_effects=True, vmem_limit_bytes=56 * 2**20
         ),
     )(harmonic_offsets, right_side, coupling, eigen_basis, eigen_inverse, eigen_size.reshape(1, NC))
+    return pl.pallas_call(
+        combine,
+        out_shape=jax.ShapeDtypeStruct((M, ROWS, KZ * R), full),
+        in_specs=[vmem, anywhere],
+        out_specs=anywhere,
+        scratch_shapes=[
+            pltpu.VMEM((M, ROWS, KZ * R), low),
+            pltpu.VMEM((M, ROWS, KZ * R), low),
+            pltpu.VMEM((M, ROWS, KZ * R), full),
+            dma((2, M)),
+            dma((M,)),
+        ],
+    )(steps, back)
 
 
 def solution(mesh):

time: 102 us -> 99.2 us (0.973)
  local copies, waits for them, and re-layouts: 3.27 us -> 0 us
    unnamed x1 -> x0, local copies, waits for them, and re-layouts: 3.27 us -> none
    pallas_call x1 -> x2, Pallas kernels: 98.9 us -> 98.5 us  [the longest x1 95.1 us: shards(): pl.pallas_call(kernel, out_shape=(jax.ShapeDtypeStruct((2, M, ROWS, KZ *...]
where the time goes in v5:
time: 99.2 us; the launch traced here: 98.5 us
  Pallas kernels  98.5 us (99%)
    pallas_call x1, Pallas kernels, shards(): pl.pallas_call(kernel, out_shape=(jax.ShapeDtypeStruct((2, M, ROWS, KZ *...  95.1 us
    pallas_call x1, Pallas kernels, shards(): pl.pallas_call(combine, out_shape=jax.ShapeDtypeStruct((M, ROWS, KZ * R),...  3.37 us

profile of v5, /device:TPU:1, one launch (start us, length us, event | category | flops | bytes accessed | tf_op | source)
XLA Modules:
  0.0 98.5 jit_solution(13468630570254637119)
XLA Ops:
  0.0 95.1 %shard_map.64 = (bf16[2,9,16,4096]{3,2,1,0:T(8,128)(2,1)}, f32[2,128]{1,0:T(2,128)}) custom-call(s32[5]{0:T(128)} %offsets.1, f32[9,16,4096]{2,1,0:T(8,128)} %right.1, bf16[9,5,256,256]{3,2,1,0:T(8,128)(2,1)} %coupling.1, bf16[256,256]{1,0:T(8,128)(2,1)} %basis.1, bf16[256,256]{1,0:T(8,128)(2,1)} %inverse.1, f32[1,256]{1,0:T(1,128)} %bitcast.1), custom_call_target="tpu_custom_call" | custom-call | tf_op jit(solution)/shard_map/pallas_call | solution.py:475
  95.1 3.4 %shard_map.65 = f32[9,16,4096]{2,1,0:T(8,128)} custom-call(f32[2,128]{1,0:T(2,128)} %get-tuple-element.7.steps, bf16[2,9,16,4096]{3,2,1,0:T(8,128)(2,1)} %get-tuple-element.8.back), custom_call_target="tpu_custom_call" | custom-call | tf_op jit(solution)/shard_map/pallas_call | solution.py:513

commit v6 on v5

--- a/solution.py
+++ b/solution.py
@@ -73,12 +73,12 @@
         to = (place + k) % (2 * NZ)
         pl.semaphore_signal(barrier, inc=1, device_id=(2 * y + to // NZ, to % NZ), device_id_type=MESH)
 
-    @pl.loop(1, NX)
+    @pl.loop(1, NX // 2)
     def _(k):
-        pl.semaphore_signal(barrier, inc=1, device_id=((sx + k) % NX, sz), device_id_type=MESH)
+        pl.semaphore_signal(barrier, inc=1, device_id=((sx + 2 * k) % NX, sz), device_id_type=MESH)
 
     pl.semaphore_signal(barrier, inc=1, device_id=across, device_id_type=MESH)
-    pl.semaphore_wait(barrier, 2 * NZ - 1 + NX - 1 + 1)
+    pl.semaphore_wait(barrier, 2 * NZ - 1 + NX // 2 - 1 + 1)
 
     def columns(index):
         return pl.ds(pl.multiple_of(index * COLS, COLS), COLS)
@@ -134,7 +134,7 @@
         )
 
     def send_mode(turn):
-        m = (turn + 3) % M
+        m = (turn + 3 * low_z) % M
 
         @pl.when(at_home)
         def _():
@@ -272,24 +272,24 @@
                 one(m)
 
     def row_copy(step, k):
-        to = (sz + k) % NZ
+        to = (place + k) % (2 * NZ)
         return pltpu.make_async_remote_copy(
             src_ref=parts.at[step],
-            dst_ref=row_sums.at[step, sz],
+            dst_ref=row_sums.at[step, place],
             send_sem=row_send.at[step],
             recv_sem=row_recv.at[step],
-            device_id=(sx, to),
+            device_id=(2 * y + to // NZ, to % NZ),
             device_id_type=MESH,
         )
 
     def all_copy(step, k):
-        to = (sx + k) % NX
+        to = (y + k) % (NX // 2)
         return pltpu.make_async_remote_copy(
             src_ref=row_total.at[step],
-            dst_ref=all_sums.at[step, sx],
+            dst_ref=all_sums.at[step, y],
             send_sem=all_send.at[step],
             recv_sem=all_recv.at[step],
-            device_id=(to, sz),
+            device_id=(2 * to + low_z, sz),
             device_id_type=MESH,
         )
 
@@ -304,34 +304,32 @@
         both = jnp.where(first_half, fold(sums[0]), fold(sums[1]))
         mine = jnp.sum(both, axis=0, keepdims=True)
         parts[step] = mine
-        row_sums[step, sz] = mine
-
-        @pl.loop(1, NZ)
+        row_sums[step, place] = mine
+
+        @pl.loop(1, 2 * NZ)
         def _(k):
             row_copy(step, k).start()
 
         send_share(step, 2)
 
-        others = row_sums.at[step, pl.ds(0, NZ - 1)]
+        others = row_sums.at[step, pl.ds(0, 2 * NZ - 1)]
         pltpu.make_async_copy(others, others, row_recv.at[step]).wait()
 
-        of_row = row_sums[step, 0]
-        for index in range(1, NZ):
-            of_row = of_row + row_sums[step, index]
+        of_row = jnp.sum(row_sums[step], axis=0)
         row_total[step] = of_row
-        all_sums[step, sx] = of_row
-
-        @pl.loop(1, NX)
+        all_sums[step, y] = of_row
+
+        @pl.loop(1, NX // 2)
         def _(k):
             all_copy(step, k).start()
 
         send_share(step, 3)
 
-        others = all_sums.at[step, pl.ds(0, NX - 1)]
+        others = all_sums.at[step, pl.ds(0, NX // 2 - 1)]
         pltpu.make_async_copy(others, others, all_recv.at[step]).wait()
 
         of_all = all_sums[step, 0]
-        for index in range(1, NX):
+        for index in range(1, NX // 2):
             of_all = of_all + all_sums[step, index]
         of_all = jnp.broadcast_to(of_all, (8, 128))
         swapped = pltpu.roll(of_all, 64, 1)
@@ -339,10 +337,21 @@
         energy = jnp.where(first_half, swapped, of_all)
         return (aligned / (energy + 1e-6))[0:1]
 
+    def sent(step):
+        others = row_sums.at[step, pl.ds(0, 2 * NZ - 1)]
+        pltpu.make_async_copy(others, others, row_send.at[step]).wait()
+        others = all_sums.at[step, pl.ds(0, NX // 2 - 1)]
+        pltpu.make_async_copy(others, others, all_send.at[step]).wait()
+
+        @pl.loop(0, OFF)
+        def _(m):
+            halo_down(step, m).wait_send()
+            halo_up(step, m + M - OFF).wait_send()
+
     def first_modes(begin, end):
         @pl.loop(begin, end)
         def _(turn):
-            m = (turn + 3) % M
+            m = (turn + 3 * core) % M
             pltpu.make_async_copy(start.at[m], start.at[m], in_recv.at[m]).wait()
 
             @pl.when(turn + WINDOW < M)
@@ -375,7 +384,7 @@
 
     @pl.loop(0, M // 3)
     def _(turn):
-        modes = [(3 * turn + 3 + each) % M for each in range(3)]
+        modes = [(3 * turn + 3 * core + each) % M for each in range(3)]
         rounded = []
         for m in modes:
             left = start[m] - first_wide * image[m]
@@ -392,23 +401,10 @@
 
     send_near(1)
     send_share(1, 0)
-    apply(1)
-    second = step_size(1)
-
-    for step in range(2):
-        pltpu.make_async_copy(back.at[step], back.at[step], out_recv.at[step]).wait()
-
-    steps[0:1, :] = first
-    steps[1:2, :] = second
-
     @pl.loop(0, M)
     def _(m):
         part = start.at[m, pl.ds(0, NC - ROWS), :]
         pltpu.make_async_copy(part, part, in_send.at[m]).wait()
-
-    for step in range(2):
-        part = search.at[step, pl.ds(OFF, M), pl.ds(0, NC - ROWS), :]
-        pltpu.make_async_copy(part, part, out_send.at[step]).wait()
 
     @pl.when(at_home)
     def _():
@@ -425,21 +421,25 @@
             for side in range(2):
                 forward(m, side).wait_send()
 
+    sent(0)
+    apply(1)
+    second = step_size(1)
+
+    for step in range(2):
+        pltpu.make_async_copy(back.at[step], back.at[step], out_recv.at[step]).wait()
+
+    steps[0:1, :] = first
+    steps[1:2, :] = second
+
+    sent(1)
+    for step in range(2):
+        part = search.at[step, pl.ds(OFF, M), pl.ds(0, NC - ROWS), :]
+        pltpu.make_async_copy(part, part, out_send.at[step]).wait()
+
+    @pl.when(away)
+    def _():
         for step in range(2):
             outward(step, 0, out_near.at[step]).wait_send()
-
-    for step in range(2):
-
-        others = row_sums.at[step, pl.ds(0, NZ - 1)]
-        pltpu.make_async_copy(others, others, row_send.at[step]).wait()
-        others = all_sums.at[step, pl.ds(0, NX - 1)]
-        pltpu.make_async_copy(others, others, all_send.at[step]).wait()
-
-        @pl.loop(0, OFF)
-        def _(m):
-            halo_down(step, m).wait_send()
-            halo_up(step, m + M - OFF).wait_send()
-
 
 def combine(steps, back, out, first, second, total, in_sem, out_sem):
     def fetch(m, step, into):
@@ -486,9 +486,9 @@
             pltpu.VMEM((2, M + 2 * OFF, NC, COLS), low),
             pltpu.VMEM((2, 8, COLS), full),
             pltpu.VMEM((2, 1, 128), full),
-            pltpu.VMEM((2, NZ, 1, 128), full),
+            pltpu.VMEM((2, 2 * NZ, 1, 128), full),
             pltpu.VMEM((2, 1, 128), full),
-            pltpu.VMEM((2, NX, 1, 128), full),
+            pltpu.VMEM((2, NX // 2, 1, 128), full),
             dma((1,)),
             dma((M,)),
             dma((M,)),

time: 99.2 us -> 98.3 us (level)
  no operation moved by 1% of the time
where the time goes in v6:
time: 98.3 us; the launch traced here: 98.1 us
  Pallas kernels  98.1 us (100%)
    pallas_call x1, Pallas kernels, shards(): pl.pallas_call(kernel, out_shape=(jax.ShapeDtypeStruct((2, M, ROWS, KZ *...  94.7 us
    pallas_call x1, Pallas kernels, shards(): pl.pallas_call(combine, out_shape=jax.ShapeDtypeStruct((M, ROWS, KZ * R),...  3.37 us

profile of v6, /device:TPU:1, one launch (start us, length us, event | category | flops | bytes accessed | tf_op | source)
XLA Modules:
  0.0 98.1 jit_solution(18070711057553749664)
XLA Ops:
  0.0 94.7 %shard_map.64 = (bf16[2,9,16,4096]{3,2,1,0:T(8,128)(2,1)}, f32[2,128]{1,0:T(2,128)}) custom-call(s32[5]{0:T(128)} %offsets.1, f32[9,16,4096]{2,1,0:T(8,128)} %right.1, bf16[9,5,256,256]{3,2,1,0:T(8,128)(2,1)} %coupling.1, bf16[256,256]{1,0:T(8,128)(2,1)} %basis.1, bf16[256,256]{1,0:T(8,128)(2,1)} %inverse.1, f32[1,256]{1,0:T(1,128)} %bitcast.1), custom_call_target="tpu_custom_call" | custom-call | tf_op jit(solution)/shard_map/pallas_call | solution.py:475
  94.7 3.4 %shard_map.65 = f32[9,16,4096]{2,1,0:T(8,128)} custom-call(f32[2,128]{1,0:T(2,128)} %get-tuple-element.7.steps, bf16[2,9,16,4096]{3,2,1,0:T(8,128)(2,1)} %get-tuple-element.8.back), custom_call_target="tpu_custom_call" | custom-call | tf_op jit(solution)/shard_map/pallas_call | solution.py:513

commit v7 on v6

--- a/solution.py
+++ b/solution.py
@@ -20,6 +20,7 @@
 QUARTER = NC // 4
 MESH = pl.DeviceIdType.MESH
 WINDOW = 4
+DIRECT = 1
 LATE = 0
 LAG = 0
 PACE = ((0, 2, 4, 4, 5), (8, 0, 4, 3, 0))
@@ -43,7 +44,7 @@
     start, factor, image, residual, blocks,
     search, sums, parts, row_sums, row_total, all_sums,
     load_sem, in_send, in_near, in_recv, out_send, out_near, out_recv, halo_send, halo_recv,
-    block_send, block_recv, pass_send, row_send, row_recv, all_send, all_recv,
+    block_send, whole_send, block_recv, pass_send, row_send, row_recv, all_send, all_recv,
 ):
     sx, sz = lax.axis_index("sx"), lax.axis_index("sz")
     y, low_z = sx // 2, sx % 2
@@ -100,6 +101,16 @@
             device_id_type=MESH,
         )
 
+    def push_whole(m, index):
+        return pltpu.make_async_remote_copy(
+            src_ref=coupling.at[m, :, quarter(index), :],
+            dst_ref=blocks.at[m, :, quarter(index), :],
+            send_sem=whole_send.at[m, index],
+            recv_sem=block_recv.at[m, index],
+            device_id=device_at(x, y, (z + 1 + 2 * (index // 2)) % 4, core),
+            device_id_type=MESH,
+        )
+
     def forward(m, side):
         index = 2 * (x % 2) + side
         return pltpu.make_async_remote_copy(
@@ -116,7 +127,7 @@
         return pltpu.make_async_copy(part, part, block_recv.at[m, index])
 
     def pass_on(m):
-        @pl.when(away)
+        @pl.when(away & (m < M - DIRECT))
         def _():
             for side in range(2):
                 arrived(m, 2 * (x % 2) + side).wait()
@@ -148,10 +159,15 @@
         def _(k):
             inward(m, k, in_send.at[m]).start()
 
-        @pl.when(at_home & (turn >= LATE))
+        @pl.when(at_home & (turn < M - DIRECT))
         def _():
             for side in range(2):
-                push(turn - LATE, side).start()
+                push(turn, side).start()
+
+        @pl.when(at_home & (turn >= M - DIRECT))
+        def _():
+            for index in range(4):
+                push_whole(turn, index).start()
 
     def outward(step, k, send_sem):
         to = (sz + k) % NZ
@@ -265,6 +281,11 @@
                     for m in modes:
                         for side in range(2):
                             arrived(m, 2 * (1 - x % 2) + side).wait()
+
+                        @pl.when(m >= M - DIRECT)
+                        def _():
+                            for side in range(2):
+                                arrived(m, 2 * (x % 2) + side).wait()
 
             for m in modes:
                 send_one(step, 1, m)
@@ -408,16 +429,24 @@
 
     @pl.when(at_home)
     def _():
-        @pl.loop(0, M)
+        @pl.loop(0, M - DIRECT)
         def _(m):
             for side in range(2):
                 push(m, side).wait_send()
+
+        @pl.loop(M - DIRECT, M)
+        def _(m):
+            for index in range(4):
+                push_whole(m, index).wait_send()
 
     @pl.when(away)
     def _():
         @pl.loop(0, M)
         def _(m):
             inward(m, 0, in_near.at[m]).wait_send()
+
+        @pl.loop(0, M - DIRECT)
+        def _(m):
             for side in range(2):
                 forward(m, side).wait_send()
 
@@ -500,6 +529,7 @@
             dma((2, 2 * OFF)),
             dma((M, 2)),
             dma((M, 4)),
+            dma((M, 4)),
             dma((M, 2)),
             dma((2,)),
             dma((2,)),

time: 98.3 us -> 96.5 us (0.982)
  Pallas kernels: 98.1 us -> 96.3 us
    pallas_call x1, Pallas kernels: 94.7 us -> 92.9 us  [shards(): pl.pallas_call(kernel, out_shape=(jax.ShapeDtypeStruct((2, M, ROWS, KZ *...]
where the time goes in v7:
time: 96.5 us; the launch traced here: 96.3 us
  Pallas kernels  96.3 us (100%)
    pallas_call x1, Pallas kernels, shards(): pl.pallas_call(kernel, out_shape=(jax.ShapeDtypeStruct((2, M, ROWS, KZ *...  92.9 us
    pallas_call x1, Pallas kernels, shards(): pl.pallas_call(combine, out_shape=jax.ShapeDtypeStruct((M, ROWS, KZ * R),...  3.37 us

profile of v7, /device:TPU:1, one launch (start us, length us, event | category | flops | bytes accessed | tf_op | source)
XLA Modules:
  0.0 96.3 jit_solution(13735661204614763603)
XLA Ops:
  0.0 92.9 %shard_map.64 = (bf16[2,9,16,4096]{3,2,1,0:T(8,128)(2,1)}, f32[2,128]{1,0:T(2,128)}) custom-call(s32[5]{0:T(128)} %offsets.1, f32[9,16,4096]{2,1,0:T(8,128)} %right.1, bf16[9,5,256,256]{3,2,1,0:T(8,128)(2,1)} %coupling.1, bf16[256,256]{1,0:T(8,128)(2,1)} %basis.1, bf16[256,256]{1,0:T(8,128)(2,1)} %inverse.1, f32[1,256]{1,0:T(1,128)} %bitcast.1), custom_call_target="tpu_custom_call" | custom-call | tf_op jit(solution)/shard_map/pallas_call | solution.py:504
  92.9 3.4 %shard_map.65 = f32[9,16,4096]{2,1,0:T(8,128)} custom-call(f32[2,128]{1,0:T(2,128)} %get-tuple-element.7.steps, bf16[2,9,16,4096]{3,2,1,0:T(8,128)(2,1)} %get-tuple-element.8.back), custom_call_target="tpu_custom_call" | custom-call | tf_op jit(solution)/shard_map/pallas_call | solution.py:543

commit v8 on v7

--- a/solution.py
+++ b/solution.py
@@ -134,7 +134,7 @@
                 forward(m, side).start()
 
     def inward(m, k, send_sem):
-        to = (group + k) % NZ
+        to = (group + (1 - core) * k + core * (NZ - k)) % NZ
         return pltpu.make_async_remote_copy(
             src_ref=right.at[m, :, columns(to)],
             dst_ref=start.at[m, rows(sz), :],
@@ -416,8 +416,8 @@
         for each, m in zip(scaled, modes):
             result = jnp.dot(basis[...], each, preferred_element_type=jnp.float32)
             search[1, OFF + m] = result.astype(jnp.bfloat16)
-        for each, m in enumerate(modes):
             send_halo(1, m)
+        for each in range(3):
             send_one(0, 4, 3 * turn + each)
 
     send_near(1)

time: 96.5 us -> 96.5 us (level)
  no operation moved by 1% of the time
where the time goes in v8:
time: 96.5 us; the launch traced here: 96.3 us
  Pallas kernels  96.3 us (100%)
    pallas_call x1, Pallas kernels, shards(): pl.pallas_call(kernel, out_shape=(jax.ShapeDtypeStruct((2, M, ROWS, KZ *...  92.9 us
    pallas_call x1, Pallas kernels, shards(): pl.pallas_call(combine, out_shape=jax.ShapeDtypeStruct((M, ROWS, KZ * R),...  3.37 us

profile of v8, /device:TPU:1, one launch (start us, length us, event | category | flops | bytes accessed | tf_op | source)
XLA Modules:
  0.0 96.3 jit_solution(12859835249861568962)
XLA Ops:
  0.0 92.9 %shard_map.64 = (bf16[2,9,16,4096]{3,2,1,0:T(8,128)(2,1)}, f32[2,128]{1,0:T(2,128)}) custom-call(s32[5]{0:T(128)} %offsets.1, f32[9,16,4096]{2,1,0:T(8,128)} %right.1, bf16[9,5,256,256]{3,2,1,0:T(8,128)(2,1)} %coupling.1, bf16[256,256]{1,0:T(8,128)(2,1)} %basis.1, bf16[256,256]{1,0:T(8,128)(2,1)} %inverse.1, f32[1,256]{1,0:T(1,128)} %bitcast.1), custom_call_target="tpu_custom_call" | custom-call | tf_op jit(solution)/shard_map/pallas_call | solution.py:504
  92.9 3.4 %shard_map.65 = f32[9,16,4096]{2,1,0:T(8,128)} custom-call(f32[2,128]{1,0:T(2,128)} %get-tuple-element.7.steps, bf16[2,9,16,4096]{3,2,1,0:T(8,128)(2,1)} %get-tuple-element.8.back), custom_call_target="tpu_custom_call" | custom-call | tf_op jit(solution)/shard_map/pallas_call | solution.py:543
